TPU v7x, 256 devices: a whole 4x4x8 slice. The times are simulated.
256 devices in a mesh: row: 32 (over z, y_hi, core), col: 8 (over y_lo, x).
Axes of the slice: x: 4, y: 4 (y_hi: 2, y_lo: 2; y = y_hi * 2 + y_lo), z: 8, core: 2. Of those that a mesh axis runs over, the one named last changes fastest.
Arguments:
- obs_summaries: bfloat16 [16384, 256], P(('row', 'col')), may hold values from -6 to 6
- sim_summaries: bfloat16 [8192, 256], P('row'), may hold values from -6 to 6
- neighbours: int32 [16384, 16], P(('row', 'col')), may hold values from 0 to 8191
- field: bfloat16 [8192, 8192], P('row', 'col'), may hold values from -6 to 6
Outputs:
- posterior: bfloat16 [16384, 8192], P('row', 'col')
Inputs may be any that keep to these rules, and one draw needn't show every extreme that they name: `neighbours`: each entry names a row of sim_summaries.
All inputs are finite; a program needn't handle non-finite values.
Results may differ from a plain program's by a relative error of at most 0.005.
Values may be sent and summed in bfloat16 or wider, within the bound.
A program may use at most 128 MiB of HBM per device.

v0:
```python
import jax
import jax.numpy as jnp
from jax import lax
from jax.sharding import PartitionSpec as P

SHARPNESS = 32.0
EPSILON = 1e-06


def neighbour_widths(obs_rows, index_rows, sims_full, sim_square):
    obs_float = obs_rows.astype(jnp.float32)
    near_rows = jnp.take(sims_full, index_rows, axis=0).astype(jnp.float32)
    inner_prod = jnp.einsum("rd,rkd->rk", obs_float, near_rows)
    obs_square = jnp.sum(obs_float * obs_float, axis=1)
    near_square = jnp.take(sim_square, index_rows, axis=0)
    distance = obs_square[:, None] + near_square - 2.0 * inner_prod
    return jnp.mean(distance, axis=1) + EPSILON


def per_device(obs_summaries, sim_summaries, neighbours, field):
    sims_full = lax.all_gather(sim_summaries, "row", axis=0, tiled=True)
    sim_float = sims_full.astype(jnp.float32)
    sim_square = jnp.sum(sim_float * sim_float, axis=1)
    obs_block = lax.all_gather(obs_summaries, "col", axis=0, tiled=True)
    index_block = lax.all_gather(neighbours, "col", axis=0, tiled=True)
    width = neighbour_widths(obs_block, index_block, sims_full, sim_square)
    obs_float = obs_block.astype(jnp.float32)
    obs_square = jnp.sum(obs_float * obs_float, axis=1)
    cross = lax.dot_general(
        obs_block, sims_full, (((1,), (1,)), ((), ())), preferred_element_type=jnp.float32
    )
    distance = obs_square[:, None] + sim_square[None, :] - 2.0 * cross
    weight = jnp.exp(-SHARPNESS * distance / width[:, None])
    numer = jnp.dot(
        weight.astype(jnp.bfloat16),
        lax.all_gather(field, "row", axis=0, tiled=True),
        preferred_element_type=jnp.float32,
    )
    total = jnp.sum(weight, axis=1)
    numer, total = (numer, total)
    return (numer / total[:, None]).astype(jnp.bfloat16)


def solution(mesh):
    return jax.shard_map(
        per_device,
        mesh=mesh,
        in_specs=(
            P(("row", "col"), None),
            P("row", None),
            P(("row", "col"), None),
            P("row", "col"),
        ),
        out_specs=P("row", "col"),
        check_vma=False,
    )
```

profile of v0, /device:TPU:8, one launch (start us, length us, event | category | flops | bytes accessed | tf_op | source)
XLA Modules:
  0.0 258.7 jit_solution(11695345352077202125)
XLA Ops:
  6.5 0.0 all-gather.4.cloned.1.call-start
  6.5 0.7 all-gather.4.cloned.1.call-update
  7.3 0.0 all-gather.6.cloned.1.call-start
  7.3 0.7 all-gather.6.cloned.1.call-update
  8.0 28.4 %all-gather = s32[8,64,16]{1,2,0:T(8,128)S(1)} all-gather(s32[1,64,16]{1,2,0:T(8,128)} %bitcast.17), channel_id=1, replica_groups=mesh['row'=32,'col'=8] {'col'}, dimensions={0}, use_global_device_ids=true | all-gather | bytes 36864 | tf_op jit(solution)/shard_map/all_gather | solution.py:25
  36.4 0.1 reshape.33
  36.5 0.1 copy.10
  36.6 0.1 reshape.14
  36.8 0.2 copy.12
  37.0 28.7 %all_gather.12 = bf16[512,256]{1,0:T(8,128)(2,1)S(1)} all-gather(bf16[64,256]{1,0:T(8,128)(2,1)} %param.4), channel_id=1, replica_groups=mesh['row'=32,'col'=8] {'col'}, dimensions={0}, use_global_device_ids=true | all-gather | bytes 294912 | tf_op jit(solution)/shard_map/all_gather | solution.py:24
  65.7 0.1 multiply_reduce_fusion.1
  65.8 33.7 %all-gather.4.cloned.1.call-done = bf16[8192,256]{1,0:T(8,128)(2,1)} async-done(((bf16[256,256]{1,0:T(8,128)(2,1)}), bf16[8192,256]{1,0:T(8,128)(2,1)}) %all-gather.4.cloned.1.call-update) | async-done | bytes 4194320 | tf_op jit(solution)/shard_map/all_gather | solution.py:21
  99.5 33.6 %gather_fusion.1 = bf16[8192,256]{1,0:T(8,128)(2,1)} fusion(bf16[8192,256]{1,0:T(8,128)(2,1)} %all-gather.4.cloned.1.call-done, s32[8192]{0:T(1024)S(1)} %broadcast_clamp_fusion), kind=kCustom, calls=%fused_computation.1 | custom fusion | bytes 8421376 | tf_op jit(solution)/shard_map/jit(_take)/gather | solution.py:12
  133.1 5.6 %fusion.2 = f32[512,1,16]{2,1,0:T(1,128)S(1)} fusion(bf16[512,16,256]{2,1,0:T(8,128)(2,1)} %bitcast.15, pred[512,16]{1,0:T(8,128)(4,1)S(1)} %copy.12, bf16[512,256,1]{1,0,2:T(8,128)(2,1)S(1)} %bitcast.16), kind=kOutput, calls=%fused_computation.6 | convolution fusion | flops 6291456 | bytes 4497408 | tf_op jit(solution)/shard_map/rd,rkd->rk/dot_general | solution.py:13
  138.7 0.1 copy.14
  138.8 3.4 %multiply_reduce_fusion = f32[8192]{0:T(1024)S(1)} fusion(bf16[8192,256]{1,0:T(8,128)(2,1)} %all-gather.4.cloned.1.call-done), kind=kLoop, calls=%fused_computation.5 | loop fusion | flops 6283264 | bytes 4227072 | tf_op jit(solution)/shard_map/reduce_sum | solution.py:23
  142.2 45.5 %gather_fusion = f32[8192]{0:T(1024)S(1)} fusion(f32[8192]{0:T(1024)S(1)} %multiply_reduce_fusion, s32[8192]{0:T(1024)S(1)} %broadcast_clamp_fusion), kind=kCustom, calls=%fused_computation | custom fusion | bytes 98304 | tf_op jit(solution)/shard_map/jit(_take)/gather | solution.py:15
  187.8 0.1 reshape.13
  187.9 0.1 copy.11
  188.0 10.0 %fusion.12 = (f32[512]{0:T(512)S(1)}, bf16[512,8192]{1,0:T(8,128)(2,1)}) fusion(f32[512]{0:T(512)S(1)} %multiply_add_fusion, bf16[512,256]{1,0:T(8,128)(2,1)S(1)} %all_gather.12, bf16[8192,256]{1,0:T(8,128)(2,1)} %all-gather.4.cloned.1.call-done, f32[8192]{0:T(1024)S(1)} %multiply_reduce_fusion, f32[512]{0:T(512)S(1)} %multiply_reduce_fusion.1), kind=kOutput, calls=%fused_computation.21 | convolution fusion | flops 2176843264 | bytes 12883968 | tf_op jit(solution)/shard_map/dot_general | solution.py:29
  198.0 38.2 %all-gather.6.cloned.1.call-done = bf16[8192,1024]{1,0:T(8,128)(2,1)} async-done(((bf16[256,1024]{1,0:T(8,128)(2,1)}), bf16[8192,1024]{1,0:T(8,128)(2,1)}) %all-gather.6.cloned.1.call-update) | async-done | bytes 16777232 | tf_op jit(solution)/shard_map/all_gather | solution.py:36
  236.2 15.6 %divide_convert_fusion = bf16[512,1024]{1,0:T(8,128)(2,1)} fusion(bf16[8192,1024]{1,0:T(8,128)(2,1)} %all-gather.6.cloned.1.call-done, bf16[512,8192]{1,0:T(8,128)(2,1)} %get-tuple-element.6, f32[512]{0:T(512)S(1)} %get-tuple-element.5), kind=kOutput, calls=%fused_computation.9 | convolution fusion | flops 8590983168 | bytes 26216448 | tf_op jit(solution)/shard_map/dot_general | solution.py:34
  (6 shorter events, 0.1 us)
Async XLA Ops:
  6.5 93.0 %all-gather.4.cloned.1.call-start = ((), (), s32[]{:S(2)}) async-start(), calls=%async_computation | async-start | bytes 4325376 | tf_op jit(solution)/shard_map/all_gather | solution.py:21
  7.3 229.0 %all-gather.6.cloned.1.call-start = ((), (), s32[]{:S(2)}) async-start(), calls=%async_computation.1 | async-start | bytes 17301504 | tf_op jit(solution)/shard_map/all_gather | solution.py:36
Sparse Core Ops, SparseCore 0:
  10.1 89.3 all-gather.3
  102.3 133.8 all-gather.5
where the time goes:
time: 261 us; the launch traced here: 259 us
  local copies, waits for them, and re-layouts  80 us (31%)
  waiting for transfers between devices  73.3 us (28%)
  blocking collectives  57.1 us (22%)
  matrix products  31.2 us (12%)
  between operations  13.5 us (5%)
  other arithmetic  3.61 us (1%)
    gather x3, local copies, waits for them, and re-layouts, neighbour_widths(): near_square = jnp.take(sim_square, index_rows, axis=0)  45.8 us
    all_gather x1, waiting for transfers between devices, per_device(): lax.all_gather(field, 'row', axis=0, tiled=True)  38.2 us
    all_gather x1, waiting for transfers between devices, per_device(): sims_full = lax.all_gather(sim_summaries, 'row', axis=0, tiled=True)  33.7 us
    gather x1, local copies, waits for them, and re-layouts, neighbour_widths(): near_rows = jnp.take(sims_full, index_rows, axis=0).astype(jnp.float32)  33.6 us
    all_gather x1, blocking collectives, per_device(): obs_block = lax.all_gather(obs_summaries, 'col', axis=0, tiled=True)  28.7 us
    all_gather x1, blocking collectives, per_device(): index_block = lax.all_gather(neighbours, 'col', axis=0, tiled=True)  28.4 us
    dot_general x1, matrix products, per_device(): jnp.dot(weight.astype(jnp.bfloat16), lax.all_gather(field, 'row', axis=0,...  15.6 us
    dot_general x1, matrix products, per_device(): lax.dot_general(obs_block, sims_full, (((1,), (1,)), ((), ())), preferred...  9.98 us
  transfers between devices with their start and end apart: 2, of which 2 were waited for; matrix products, arithmetic and copies ran while one was open for 38% of the time, Pallas kernels for 0%

commit v1 on v0

v1 whole, which is shorter than its diff:
```python
import jax
import jax.numpy as jnp
import numpy as np
from jax import lax
from jax.sharding import Mesh
from jax.sharding import PartitionSpec as P

SHARPNESS = 32.0
EPSILON = 1e-06
ROWS = ("z", "yh", "core")
COLS = ("yl", "x")


def per_device(obs_summaries, sim_summaries, neighbours, field):
    sim_dev = sim_summaries.shape[0]
    n_chip = lax.psum(1, ("z", "yh"))
    sims_chip = lax.all_gather(sim_summaries, ("z", "yh"), axis=0, tiled=True)
    sims_full = lax.all_gather(sims_chip, "core", axis=0, tiled=True)
    field_chip = lax.all_gather(field, ("z", "yh"), axis=0, tiled=True)
    field_full = lax.all_gather(field_chip, "core", axis=0, tiled=True)
    obs_block = lax.all_gather(obs_summaries, COLS, axis=0, tiled=True)
    index_block = lax.all_gather(neighbours, COLS, axis=0, tiled=True)

    sim_float = sims_full.astype(jnp.float32)
    sim_square = jnp.sum(sim_float * sim_float, axis=1)
    obs_float = obs_block.astype(jnp.float32)
    obs_square = jnp.sum(obs_float * obs_float, axis=1)
    cross = lax.dot_general(
        obs_block, sims_full, (((1,), (1,)), ((), ())), preferred_element_type=jnp.float32
    )
    distance = obs_square[:, None] + sim_square[None, :] - 2.0 * cross

    within = index_block % sim_dev
    owner = index_block // sim_dev
    place = (owner % 2) * (n_chip * sim_dev) + (owner // 2) * sim_dev + within
    near = jnp.take_along_axis(distance, place, axis=1)
    width = jnp.mean(near, axis=1) + EPSILON

    weight = jnp.exp(-SHARPNESS * distance / width[:, None])
    numer = jnp.dot(weight.astype(jnp.bfloat16), field_full, preferred_element_type=jnp.float32)
    total = jnp.sum(weight, axis=1)
    return (numer / total[:, None]).astype(jnp.bfloat16)


def solution(mesh):
    n_row, n_col = mesh.devices.shape
    fine = Mesh(mesh.devices.reshape(n_row // 4, 2, 2, 2, n_col // 2), ROWS + COLS)
    return jax.shard_map(
        per_device,
        mesh=fine,
        in_specs=(
            P(ROWS + COLS, None),
            P(ROWS, None),
            P(ROWS + COLS, None),
            P(ROWS, COLS),
        ),
        out_specs=P(ROWS, COLS),
        check_vma=False,
    )
```

time: 261 us -> 443 us (1.70)
  waiting for transfers between devices: 73.3 us -> 226 us
  local copies, waits for them, and re-layouts: 80 us -> 104 us
  other arithmetic: 3.61 us -> 11.2 us
    all_gather x2 -> x4, waiting for transfers between devices: 71.9 us -> 225 us  [the longest x1 135 us: per_device(): field_chip = lax.all_gather(field, ('z', 'yh'), axis=0, tiled=True)]
    gather x4 -> x5, local copies, waits for them, and re-layouts: 79.3 us -> 103 us  [per_device(): near = jnp.take_along_axis(distance, place, axis=1)]
    reduce_sum x1 -> x2, other arithmetic: 0.04 us -> 7.66 us  [the longest x1 7.63 us: per_device(): total = jnp.sum(weight, axis=1)]
    dot_general x2 -> x1, matrix products: 21.2 us -> 18.2 us  [per_device(): jnp.dot(weight.astype(jnp.bfloat16), field_full, preferred_element_type=j...]
  transfers between devices with their start and end apart: 2 -> 4, of which waited for: 2 -> 2; matrix products, arithmetic and copies ran while one was open for 38% -> 28% of each run, Pallas kernels for 0% -> 0%
where the time goes in v1:
time: 443 us; the launch traced here: 439 us
  waiting for transfers between devices  226 us (51%)
  local copies, waits for them, and re-layouts  104 us (23%)
  blocking collectives  57.3 us (13%)
  matrix products  27.4 us (6%)
  between operations  13.2 us (3%)
  other arithmetic  11.2 us (3%)
    all_gather x1, waiting for transfers between devices, per_device(): field_chip = lax.all_gather(field, ('z', 'yh'), axis=0, tiled=True)  135 us
    gather x5, local copies, waits for them, and re-layouts, per_device(): near = jnp.take_along_axis(distance, place, axis=1)  103 us
    all_gather x1, waiting for transfers between devices, per_device(): sims_chip = lax.all_gather(sim_summaries, ('z', 'yh'), axis=0, tiled=True)  89.4 us
    all_gather x1, blocking collectives, per_device(): obs_block = lax.all_gather(obs_summaries, COLS, axis=0, tiled=True)  28.7 us
    all_gather x1, blocking collectives, per_device(): index_block = lax.all_gather(neighbours, COLS, axis=0, tiled=True)  28.6 us
    dot_general x1, matrix products, per_device(): jnp.dot(weight.astype(jnp.bfloat16), field_full, preferred_element_type=j...  18.2 us
    dot_general x1, matrix products, per_device(): lax.dot_general(obs_block, sims_full, (((1,), (1,)), ((), ())), preferred...  9.22 us
  transfers between devices with their start and end apart: 4, of which 2 were waited for; matrix products, arithmetic and copies ran while one was open for 28% of the time, Pallas kernels for 0%

profile of v1, /device:TPU:8, one launch (start us, length us, event | category | flops | bytes accessed | tf_op | source)
XLA Modules:
  0.0 438.8 jit_solution(13162314872903564946)
XLA Ops:
  6.5 0.7 all-gather.6.cloned.1.call-update
  7.3 0.0 all-gather.10.cloned.1.call-start
  7.3 0.7 all-gather.10.cloned.1.call-update
  8.0 0.0 all-gather.8.cloned.1.call-start
  8.1 89.4 %all-gather.6.cloned.1.call-done = bf16[4096,256]{1,0:T(8,128)(2,1)} async-done(((bf16[256,256]{1,0:T(8,128)(2,1)}), bf16[4096,256]{1,0:T(8,128)(2,1)}) %all-gather.6.cloned.1.call-update) | async-done | bytes 2097168 | tf_op jit(solution)/shard_map/all_gather | solution.py:17
  97.5 0.0 all-gather.8.cloned.1.call-update
  97.5 0.0 all-gather.12.cloned.1.call-start
  97.5 135.1 %all-gather.10.cloned.1.call-done = bf16[4096,1024]{1,0:T(8,128)(2,1)} async-done(((bf16[256,1024]{1,0:T(8,128)(2,1)}), bf16[4096,1024]{1,0:T(8,128)(2,1)}) %all-gather.10.cloned.1.call-update) | async-done | bytes 8388624 | tf_op jit(solution)/shard_map/all_gather | solution.py:19
  232.6 28.6 %all-gather = s32[8,64,16]{1,2,0:T(8,128)S(1)} all-gather(s32[1,64,16]{1,2,0:T(8,128)} %bitcast.10), channel_id=1, replica_groups=mesh['z'=8,'yh'=2,'core'=2,'yl'=2,'x'=4] {'yl','x'}, dimensions={0}, use_global_device_ids=true | all-gather | bytes 36864 | tf_op jit(solution)/shard_map/all_gather | solution.py:22
  261.3 0.1 reshape.29
  261.4 0.1 bitcast_or_fusion
  261.5 0.1 copy.9
  261.6 0.1 reshape.17
  261.7 28.7 %all_gather.18 = bf16[512,256]{1,0:T(8,128)(2,1)S(1)} all-gather(bf16[64,256]{1,0:T(8,128)(2,1)} %param.4), channel_id=1, replica_groups=mesh['z'=8,'yh'=2,'core'=2,'yl'=2,'x'=4] {'yl','x'}, dimensions={0}, use_global_device_ids=true | all-gather | bytes 294912 | tf_op jit(solution)/shard_map/all_gather | solution.py:21
  290.4 0.1 multiply_reduce_fusion.1
  290.6 0.0 all-gather.8.cloned.1.call-done
  290.6 3.3 multiply_reduce_fusion
  293.9 9.2 %multiply_subtract_fusion = f32[512,8192]{1,0:T(8,128)} fusion(bf16[512,256]{1,0:T(8,128)(2,1)S(1)} %all_gather.18, bf16[8192,256]{1,0:T(8,128)(2,1)} %all-gather.8.cloned.1.call-done, f32[8192]{0:T(1024)S(1)} %multiply_reduce_fusion, f32[512]{0:T(512)S(1)} %multiply_reduce_fusion.1), kind=kOutput, calls=%fused_computation.2 | convolution fusion | flops 2160066560 | bytes 21268480 | tf_op jit(solution)/shard_map/dot_general | solution.py:28
  303.2 103.0 %gather_fusion = f32[8192]{0:T(1024)S(1)} fusion(f32[512,8192]{1,0:T(8,128)} %multiply_subtract_fusion, s32[8192]{0:T(1024)S(1)} %reshape.17), kind=kCustom, calls=%fused_computation | custom fusion | bytes 131072 | tf_op jit(solution)/shard_map/jit(take_along_axis)/gather | solution.py:36
  406.2 0.1 reshape.20
  406.3 0.1 copy.10
  406.5 7.6 %fusion.4 = f32[512]{0:T(512)S(1)} fusion(f32[512]{0:T(512)S(1)} %multiply_add_fusion, f32[512,8192]{1,0:T(8,128)} %multiply_subtract_fusion), kind=kLoop, calls=%fused_computation.7 | loop fusion | flops 12582400 | bytes 16781312 | tf_op jit(solution)/shard_map/reduce_sum | solution.py:41
  414.1 0.0 all-gather.12.cloned.1.call-done
  414.1 18.2 %divide_convert_fusion = bf16[512,1024]{1,0:T(8,128)(2,1)} fusion(bf16[8192,1024]{1,0:T(8,128)(2,1)} %all-gather.12.cloned.1.call-done, f32[512]{0:T(512)S(1)} %fusion.4, f32[512,8192]{1,0:T(8,128)} %multiply_subtract_fusion, f32[512]{0:T(512)S(1)} %multiply_add_fusion), kind=kOutput, calls=%fused_computation.6 | convolution fusion | flops 8603566080 | bytes 34607104 | tf_op jit(solution)/shard_map/dot_general | solution.py:40
  (5 shorter events, 0.1 us)
Async XLA Ops:
  6.5 90.9 %all-gather.6.cloned.1.call-start = ((), (), s32[]{:S(2)}) async-start(), calls=%async_computation | async-start | bytes 2228224 | tf_op jit(solution)/shard_map/all_gather | solution.py:17
  7.3 225.4 %all-gather.10.cloned.1.call-start = ((), (), s32[]{:S(2)}) async-start(), calls=%async_computation.2 | async-start | bytes 8912896 | tf_op jit(solution)/shard_map/all_gather | solution.py:19
  8.0 282.6 %all-gather.8.cloned.1.call-start = ((), (), s32[]{:S(2)}) async-start(), calls=%async_computation.1 | async-start | bytes 6291456 | tf_op jit(solution)/shard_map/all_gather | solution.py:18
  97.5 316.6 %all-gather.12.cloned.1.call-start = ((), (), s32[]{:S(2)}) async-start(), calls=%async_computation.3 | async-start | bytes 25165824 | tf_op jit(solution)/shard_map/all_gather | solution.py:20
Sparse Core Ops, SparseCore 0:
  9.9 87.4 all-gather.5
  100.1 132.4 all-gather.9
  234.4 16.6 all-gather.7
  252.8 36.6 all-gather.11

commit v2 on v1

v2 whole, which is shorter than its diff:
```python
import functools

import jax
import jax.numpy as jnp
from jax import lax
from jax.experimental import pallas as pl
from jax.experimental.pallas import tpu as pltpu
from jax.sharding import Mesh
from jax.sharding import PartitionSpec as P

SHARPNESS = 32.0
EPSILON = 1e-06
ROWS = ("z", "yh", "core")
COLS = ("yl", "x")
MESH = pl.DeviceIdType.MESH


def ring_device(pos, n_z, lane):
    chip = pos // 2
    core = pos % 2
    start = lane * (n_z // 2)
    low = chip < n_z
    z = jnp.where(low, (start + chip) % n_z, (start + 2 * n_z - 1 - chip) % n_z)
    yh = jnp.where(low, 0, 1)
    return z, yh, core


def ring_gather_kernel(n_z, field_ref, sims_ref, field_out, sims_out, send_sem, recv_sem, local_sem):
    z = lax.axis_index("z")
    yh = lax.axis_index("yh")
    core = lax.axis_index("core")
    yl = lax.axis_index("yl")
    x = lax.axis_index("x")
    n = 4 * n_z
    start = yl * (n_z // 2)
    rel = (z - start + n_z) % n_z
    chip = jnp.where(yh == 0, rel, 2 * n_z - 1 - rel)
    pos = 2 * chip + core
    me = (z * 2 + yh) * 2 + core

    def dev(p):
        dz, dyh, dcore = ring_device(p, n_z, yl)
        return (dz, dyh, dcore, yl, x)

    def origin(p):
        dz, dyh, dcore = ring_device(p, n_z, yl)
        return (dz * 2 + dyh) * 2 + dcore

    right = dev((pos + 1) % n)
    left = dev((pos + n - 1) % n)

    barrier = pltpu.get_barrier_semaphore()
    pl.semaphore_signal(barrier, inc=1, device_id=left, device_id_type=MESH)
    pl.semaphore_signal(barrier, inc=1, device_id=right, device_id_type=MESH)
    pl.semaphore_wait(barrier, 2)

    local = [
        pltpu.make_async_copy(field_ref, field_out.at[me], local_sem.at[0]),
        pltpu.make_async_copy(sims_ref, sims_out.at[me], local_sem.at[1]),
    ]
    for c in local:
        c.start()

    n_fwd = n // 2
    n_bwd = n - 1 - n_fwd
    copies = []

    def hop(direction, step, target):
        if direction == 0:
            src_pos = (pos - step + 1 + n) % n
        else:
            src_pos = (pos + step - 1) % n
        o = origin(src_pos)
        made = []
        for k, (src_in, out) in enumerate(((field_ref, field_out), (sims_ref, sims_out))):
            src = src_in if step == 1 else out.at[o]
            made.append(
                pltpu.make_async_remote_copy(
                    src_ref=src,
                    dst_ref=out.at[o],
                    send_sem=send_sem.at[direction, k, step - 1],
                    recv_sem=recv_sem.at[direction, k, step - 1],
                    device_id=target,
                    device_id_type=MESH,
                )
            )
        return made

    prev = {0: None, 1: None}
    for step in range(1, n_fwd + 1):
        for direction, count, target in ((0, n_fwd, right), (1, n_bwd, left)):
            if step > count:
                continue
            if prev[direction] is not None:
                for c in prev[direction]:
                    c.wait_recv()
            made = hop(direction, step, target)
            for c in made:
                c.start()
            copies.extend(made)
            prev[direction] = made
    for direction in (0, 1):
        for c in prev[direction]:
            c.wait_recv()
    for c in copies:
        c.wait_send()
    for c in local:
        c.wait()


def ring_gather(field, sims, n_z):
    n = 4 * n_z
    n_fwd = n // 2
    return pl.pallas_call(
        functools.partial(ring_gather_kernel, n_z),
        out_shape=(
            jax.ShapeDtypeStruct((n,) + field.shape, field.dtype),
            jax.ShapeDtypeStruct((n,) + sims.shape, sims.dtype),
        ),
        in_specs=[pl.BlockSpec(memory_space=pl.ANY)] * 2,
        out_specs=(pl.BlockSpec(memory_space=pl.ANY), pl.BlockSpec(memory_space=pl.ANY)),
        scratch_shapes=[
            pltpu.SemaphoreType.DMA((2, 2, n_fwd)),
            pltpu.SemaphoreType.DMA((2, 2, n_fwd)),
            pltpu.SemaphoreType.DMA((2,)),
        ],
        compiler_params=pltpu.CompilerParams(collective_id=0, has_side_effects=True),
    )(field, sims)


def per_device(n_z, obs_summaries, sim_summaries, neighbours, field):
    field_all, sims_all = ring_gather(field, sim_summaries, n_z)
    field_full = field_all.reshape(-1, field.shape[1])
    sims_full = sims_all.reshape(-1, sim_summaries.shape[1])
    obs_block = lax.all_gather(obs_summaries, COLS, axis=0, tiled=True)
    index_block = lax.all_gather(neighbours, COLS, axis=0, tiled=True)

    sim_float = sims_full.astype(jnp.float32)
    sim_square = jnp.sum(sim_float * sim_float, axis=1)
    obs_float = obs_block.astype(jnp.float32)
    obs_square = jnp.sum(obs_float * obs_float, axis=1)
    cross = lax.dot_general(
        obs_block, sims_full, (((1,), (1,)), ((), ())), preferred_element_type=jnp.float32
    )
    distance = obs_square[:, None] + sim_square[None, :] - 2.0 * cross

    sim_ids = lax.broadcasted_iota(jnp.int32, (1, 1, sims_full.shape[0]), 2)
    counts = jnp.sum((index_block[:, :, None] == sim_ids).astype(jnp.float32), axis=1)
    width = jnp.sum(counts * distance, axis=1) / index_block.shape[1] + EPSILON

    weight = jnp.exp(-SHARPNESS * distance / width[:, None])
    numer = jnp.dot(weight.astype(jnp.bfloat16), field_full, preferred_element_type=jnp.float32)
    total = jnp.sum(weight, axis=1)
    return (numer / total[:, None]).astype(jnp.bfloat16)


def solution(mesh):
    n_row, n_col = mesh.devices.shape
    n_z = n_row // 4
    fine = Mesh(mesh.devices.reshape(n_z, 2, 2, 2, n_col // 2), ROWS + COLS)
    return jax.shard_map(
        functools.partial(per_device, n_z),
        mesh=fine,
        in_specs=(
            P(ROWS + COLS, None),
            P(ROWS, None),
            P(ROWS + COLS, None),
            P(ROWS, COLS),
        ),
        out_specs=P(ROWS, COLS),
        check_vma=False,
    )
```

time: 443 us -> 314 us (0.71)
  waiting for transfers between devices: 226 us -> 0 us
  Pallas kernels: 0 us -> 121 us
  local copies, waits for them, and re-layouts: 104 us -> 17.6 us
  other arithmetic: 11.2 us -> 84.6 us
  between operations: 13.2 us -> 0.05 us
  matrix products: 27.4 us -> 33.4 us
    all_gather x4 -> x0, waiting for transfers between devices: 225 us -> none  [the longest x1 135 us: per_device(): field_chip = lax.all_gather(field, ('z', 'yh'), axis=0, tiled=True)]
    pallas_call x0 -> x1, Pallas kernels: none -> 121 us  [ring_gather(): pl.pallas_call(functools.partial(ring_gather_kernel, n_z), out_shape=(jax...]
    gather x5 -> x0, local copies, waits for them, and re-layouts: 103 us -> none  [per_device(): near = jnp.take_along_axis(distance, place, axis=1)]
    reduce_sum x1, other arithmetic: 0.03 us -> 72.7 us  [per_device(): jnp.sum((index_block[:, :, None] == sim_ids).astype(jnp.float32), axis=1)]
    reduce_sum x0 -> x1, local copies, waits for them, and re-layouts: none -> 17.5 us  [per_device(): jnp.sum((index_block[:, :, None] == sim_ids).astype(jnp.float32), axis=1)]
  transfers between devices with their start and end apart: 4 -> 0, of which waited for: 2 -> 0; matrix products, arithmetic and copies ran while one was open for 28% -> 0% of each run, Pallas kernels for 0% -> 0%
where the time goes in v2:
time: 314 us
  Pallas kernels  121 us (39%)
  other arithmetic  84.6 us (27%)
  blocking collectives  57 us (18%)
  matrix products  33.4 us (11%)
  local copies, waits for them, and re-layouts  17.6 us (6%)
    pallas_call x1, Pallas kernels, ring_gather(): pl.pallas_call(functools.partial(ring_gather_kernel, n_z), out_shape=(jax...  121 us
    reduce_sum x1, other arithmetic, per_device(): jnp.sum((index_block[:, :, None] == sim_ids).astype(jnp.float32), axis=1)  72.7 us
    all_gather x1, blocking collectives, per_device(): obs_block = lax.all_gather(obs_summaries, COLS, axis=0, tiled=True)  28.6 us
    all_gather x1, blocking collectives, per_device(): index_block = lax.all_gather(neighbours, COLS, axis=0, tiled=True)  28.3 us
    dot_general x1, matrix products, per_device(): jnp.dot(weight.astype(jnp.bfloat16), field_full, preferred_element_type=j...  20.5 us
    reduce_sum x1, local copies, waits for them, and re-layouts, per_device(): jnp.sum((index_block[:, :, None] == sim_ids).astype(jnp.float32), axis=1)  17.5 us
    dot_general x1, matrix products, per_device(): lax.dot_general(obs_block, sims_full, (((1,), (1,)), ((), ())), preferred...  12.9 us
    reduce_sum x1, other arithmetic, per_device(): total = jnp.sum(weight, axis=1)  8.4 us

profile of v2, /device:TPU:8, one launch (start us, length us, event | category | flops | bytes accessed | tf_op | source)
XLA Modules:
  0.0 313.8 jit_solution(14496999333805916395)
XLA Ops:
  0.0 28.3 %all-gather = s32[8,64,16]{1,2,0:T(8,128)S(1)} all-gather(s32[1,64,16]{1,2,0:T(8,128)} %bitcast.26), channel_id=1, replica_groups=mesh['z'=8,'yh'=2,'core'=2,'yl'=2,'x'=4] {'yl','x'}, dimensions={0}, use_global_device_ids=true | all-gather | bytes 36864 | tf_op jit(solution)/shard_map/all_gather | solution.py:136
  28.4 0.1 copy.12
  28.5 28.6 %all_gather.6 = bf16[512,256]{1,0:T(8,128)(2,1)S(1)} all-gather(bf16[64,256]{1,0:T(8,128)(2,1)} %param.4), channel_id=1, replica_groups=mesh['z'=8,'yh'=2,'core'=2,'yl'=2,'x'=4] {'yl','x'}, dimensions={0}, use_global_device_ids=true | all-gather | bytes 294912 | tf_op jit(solution)/shard_map/all_gather | solution.py:135
  57.1 0.1 multiply_reduce_fusion.2
  57.2 72.7 %convert_reduce_fusion = f32[512,8192]{1,0:T(8,128)} fusion(s32[512,16]{1,0:T(8,128)S(1)} %bitcast.21), kind=kLoop, calls=%fused_computation | loop fusion | flops 197132288 | bytes 16809984 | tf_op jit(solution)/shard_map/reduce_sum | solution.py:148
  129.9 17.5 %copy.11 = f32[512,8192]{0,1:T(8,128)} copy(f32[512,8192]{1,0:T(8,128)} %convert_reduce_fusion) | data formatting | bytes 33554432 | tf_op jit(solution)/shard_map/reduce_sum | solution.py:148
  147.4 121.2 %shard_map.46 = (bf16[32,256,1024]{2,1,0:T(8,128)(2,1)}, bf16[32,256,256]{2,1,0:T(8,128)(2,1)}) custom-call(bf16[256,1024]{1,0:T(8,128)(2,1)} %field_ref.1, bf16[256,256]{1,0:T(8,128)(2,1)} %sims_ref.1), custom_call_target="tpu_custom_call" | custom-call | tf_op jit(solution)/shard_map/pallas_call | solution.py:114
  268.5 3.3 %multiply_reduce_fusion.1 = f32[32,256]{1,0:T(8,128)S(1)} fusion(bf16[32,256,256]{2,1,0:T(8,128)(2,1)} %get-tuple-element.7), kind=kLoop, calls=%fused_computation.7 | loop fusion | flops 6283264 | bytes 4227072 | tf_op jit(solution)/shard_map/reduce_sum | solution.py:139
  271.9 12.9 %multiply_reduce_fusion = (f32[512]{0:T(512)S(1)}, f32[8192,512]{1,0:T(8,128)}) fusion(f32[512,8192]{0,1:T(8,128)} %copy.11, f32[8192]{0:T(1024)S(1)} %bitcast.22, f32[512]{0:T(512)S(1)} %multiply_reduce_fusion.2, bf16[8192,256]{1,0:T(8,128)(2,1)} %bitcast.20, bf16[512,256]{1,0:T(8,128)(2,1)S(1)} %all_gather.6), kind=kOutput, calls=%fused_computation.4 | convolution fusion | flops 2168454656 | bytes 38047744 | tf_op jit(solution)/shard_map/dot_general | solution.py:142
  284.8 8.4 %fusion.4 = f32[512]{0:T(512)S(1)} fusion(f32[512]{0:T(512)S(1)} %multiply_add_fusion, f32[8192,512]{1,0:T(8,128)} %get-tuple-element.10, f32[8192]{0:T(1024)S(1)} %bitcast.23, f32[512]{0:T(512)S(1)} %multiply_reduce_fusion.2), kind=kLoop, calls=%fused_computation.11 | loop fusion | flops 25165312 | bytes 16816128 | tf_op jit(solution)/shard_map/reduce_sum | solution.py:153
  293.2 20.5 %divide_convert_fusion = bf16[512,1024]{1,0:T(8,128)(2,1)} fusion(bf16[8192,1024]{1,0:T(8,128)(2,1)} %bitcast.27, f32[512]{0:T(512)S(1)} %fusion.4, f32[8192,512]{1,0:T(8,128)} %get-tuple-element.10, f32[512]{0:T(512)S(1)} %multiply_add_fusion, f32[8192]{0:T(1024)S(1)} %bitcast.24, f32[512]{0:T(512)S(1)} %multiply_reduce_fusion.2), kind=kOutput, calls=%fused_computation.8 | convolution fusion | flops 8616148992 | bytes 34641920 | tf_op jit(solution)/shard_map/dot_general | solution.py:152
  (2 shorter events, 0.0 us)

commit v3 on v2

--- a/solution.py
+++ b/solution.py
@@ -25,7 +25,15 @@
     return z, yh, core
 
 
-def ring_gather_kernel(n_z, field_ref, sims_ref, field_out, sims_out, send_sem, recv_sem, local_sem):
+def col_peers(n_x, yl, x):
+    me = yl * n_x + x
+    return me, [((me + d) % (2 * n_x)) for d in range(1, 2 * n_x)]
+
+
+def ring_gather_kernel(
+    n_z, field_ref, sims_ref, obs_ref, nbr_ref, field_out, sims_out, obs_out, nbr_out,
+    send_sem, recv_sem, local_sem, col_send, col_recv,
+):
     z = lax.axis_index("z")
     yh = lax.axis_index("yh")
     core = lax.axis_index("core")
@@ -49,16 +57,37 @@
     right = dev((pos + 1) % n)
     left = dev((pos + n - 1) % n)
 
+    n_x = obs_out.shape[0] // 2
+    mine, peers = col_peers(n_x, yl, x)
+    peer_devs = [(z, yh, core, p // n_x, p % n_x) for p in peers]
+
     barrier = pltpu.get_barrier_semaphore()
-    pl.semaphore_signal(barrier, inc=1, device_id=left, device_id_type=MESH)
-    pl.semaphore_signal(barrier, inc=1, device_id=right, device_id_type=MESH)
-    pl.semaphore_wait(barrier, 2)
+    for d in [left, right] + peer_devs:
+        pl.semaphore_signal(barrier, inc=1, device_id=d, device_id_type=MESH)
+    pl.semaphore_wait(barrier, 2 + len(peer_devs))
 
     local = [
         pltpu.make_async_copy(field_ref, field_out.at[me], local_sem.at[0]),
         pltpu.make_async_copy(sims_ref, sims_out.at[me], local_sem.at[1]),
+        pltpu.make_async_copy(obs_ref, obs_out.at[mine], local_sem.at[2]),
+        pltpu.make_async_copy(nbr_ref, nbr_out.at[mine], local_sem.at[3]),
     ]
     for c in local:
+        c.start()
+    col_copies = []
+    for i, d in enumerate(peer_devs):
+        for k, (src, out) in enumerate(((obs_ref, obs_out), (nbr_ref, nbr_out))):
+            col_copies.append(
+                pltpu.make_async_remote_copy(
+                    src_ref=src,
+                    dst_ref=out.at[mine],
+                    send_sem=col_send.at[k, i],
+                    recv_sem=col_recv.at[k, mine],
+                    device_id=d,
+                    device_id_type=MESH,
+                )
+            )
+    for c in col_copies:
         c.start()
 
     n_fwd = n // 2
@@ -102,13 +131,23 @@
     for direction in (0, 1):
         for c in prev[direction]:
             c.wait_recv()
-    for c in copies:
+    for p in peers:
+        for k, out in enumerate((obs_out, nbr_out)):
+            pltpu.make_async_remote_copy(
+                src_ref=out.at[p],
+                dst_ref=out.at[p],
+                send_sem=col_send.at[k, 0],
+                recv_sem=col_recv.at[k, p],
+                device_id=peer_devs[0],
+                device_id_type=MESH,
+            ).wait_recv()
+    for c in copies + col_copies:
         c.wait_send()
     for c in local:
         c.wait()
 
 
-def ring_gather(field, sims, n_z):
+def ring_gather(field, sims, obs, nbr, n_z, n_col):
     n = 4 * n_z
     n_fwd = n // 2
     return pl.pallas_call(
@@ -116,24 +155,97 @@
         out_shape=(
             jax.ShapeDtypeStruct((n,) + field.shape, field.dtype),
             jax.ShapeDtypeStruct((n,) + sims.shape, sims.dtype),
+            jax.ShapeDtypeStruct((n_col,) + obs.shape, obs.dtype),
+            jax.ShapeDtypeStruct((n_col,) + nbr.shape, nbr.dtype),
         ),
-        in_specs=[pl.BlockSpec(memory_space=pl.ANY)] * 2,
-        out_specs=(pl.BlockSpec(memory_space=pl.ANY), pl.BlockSpec(memory_space=pl.ANY)),
+        in_specs=[pl.BlockSpec(memory_space=pl.ANY)] * 4,
+        out_specs=tuple(pl.BlockSpec(memory_space=pl.ANY) for _ in range(4)),
         scratch_shapes=[
             pltpu.SemaphoreType.DMA((2, 2, n_fwd)),
             pltpu.SemaphoreType.DMA((2, 2, n_fwd)),
-            pltpu.SemaphoreType.DMA((2,)),
+            pltpu.SemaphoreType.DMA((4,)),
+            pltpu.SemaphoreType.DMA((2, n_col - 1)),
+            pltpu.SemaphoreType.DMA((2, n_col)),
         ],
         compiler_params=pltpu.CompilerParams(collective_id=0, has_side_effects=True),
-    )(field, sims)
+    )(field, sims, obs, nbr)
+
+
+def col_gather_kernel(val_ref, out_ref, send_sem, recv_sem, local_sem):
+    z = lax.axis_index("z")
+    yh = lax.axis_index("yh")
+    core = lax.axis_index("core")
+    yl = lax.axis_index("yl")
+    x = lax.axis_index("x")
+    n_x = out_ref.shape[0] // 2
+    mine, peers = col_peers(n_x, yl, x)
+    peer_devs = [(z, yh, core, p // n_x, p % n_x) for p in peers]
+    barrier = pltpu.get_barrier_semaphore()
+    for d in peer_devs:
+        pl.semaphore_signal(barrier, inc=1, device_id=d, device_id_type=MESH)
+    pl.semaphore_wait(barrier, len(peer_devs))
+    local = pltpu.make_async_copy(val_ref, out_ref.at[mine], local_sem.at[0])
+    local.start()
+    sent = []
+    for i, d in enumerate(peer_devs):
+        c = pltpu.make_async_remote_copy(
+            src_ref=val_ref,
+            dst_ref=out_ref.at[mine],
+            send_sem=send_sem.at[i],
+            recv_sem=recv_sem.at[mine],
+            device_id=d,
+            device_id_type=MESH,
+        )
+        c.start()
+        sent.append(c)
+    for p in peers:
+        pltpu.make_async_remote_copy(
+            src_ref=out_ref.at[p],
+            dst_ref=out_ref.at[p],
+            send_sem=send_sem.at[0],
+            recv_sem=recv_sem.at[p],
+            device_id=peer_devs[0],
+            device_id_type=MESH,
+        ).wait_recv()
+    for c in sent:
+        c.wait_send()
+    local.wait()
+
+
+def col_gather(val, n_col):
+    return pl.pallas_call(
+        col_gather_kernel,
+        out_shape=jax.ShapeDtypeStruct((n_col,) + val.shape, val.dtype),
+        in_specs=[pl.BlockSpec(memory_space=pl.ANY)],
+        out_specs=pl.BlockSpec(memory_space=pl.ANY),
+        scratch_shapes=[
+            pltpu.SemaphoreType.DMA((n_col - 1,)),
+            pltpu.SemaphoreType.DMA((n_col,)),
+            pltpu.SemaphoreType.DMA((1,)),
+        ],
+        compiler_params=pltpu.CompilerParams(collective_id=1, has_side_effects=True),
+    )(val)
+
+
+def neighbour_widths(obs_rows, index_rows, sims_full):
+    obs_float = obs_rows.astype(jnp.float32)
+    near_rows = jnp.take(sims_full, index_rows, axis=0).astype(jnp.float32)
+    inner_prod = jnp.einsum("rd,rkd->rk", obs_float, near_rows)
+    obs_square = jnp.sum(obs_float * obs_float, axis=1)
+    near_square = jnp.sum(near_rows * near_rows, axis=2)
+    distance = obs_square[:, None] + near_square - 2.0 * inner_prod
+    return jnp.mean(distance, axis=1) + EPSILON
 
 
 def per_device(n_z, obs_summaries, sim_summaries, neighbours, field):
-    field_all, sims_all = ring_gather(field, sim_summaries, n_z)
+    n_col = 2 * lax.psum(1, "x")
+    field_all, sims_all, obs_all, _ = ring_gather(field, sim_summaries, obs_summaries, neighbours, n_z, n_col)
     field_full = field_all.reshape(-1, field.shape[1])
     sims_full = sims_all.reshape(-1, sim_summaries.shape[1])
-    obs_block = lax.all_gather(obs_summaries, COLS, axis=0, tiled=True)
-    index_block = lax.all_gather(neighbours, COLS, axis=0, tiled=True)
+    obs_block = obs_all.reshape(-1, obs_summaries.shape[1])
+
+    own_width = neighbour_widths(obs_summaries, neighbours, sims_full)
+    width = col_gather(own_width.reshape(1, -1), n_col).reshape(-1)
 
     sim_float = sims_full.astype(jnp.float32)
     sim_square = jnp.sum(sim_float * sim_float, axis=1)
@@ -143,10 +255,6 @@
         obs_block, sims_full, (((1,), (1,)), ((), ())), preferred_element_type=jnp.float32
     )
     distance = obs_square[:, None] + sim_square[None, :] - 2.0 * cross
-
-    sim_ids = lax.broadcasted_iota(jnp.int32, (1, 1, sims_full.shape[0]), 2)
-    counts = jnp.sum((index_block[:, :, None] == sim_ids).astype(jnp.float32), axis=1)
-    width = jnp.sum(counts * distance, axis=1) / index_block.shape[1] + EPSILON
 
     weight = jnp.exp(-SHARPNESS * distance / width[:, None])
     numer = jnp.dot(weight.astype(jnp.bfloat16), field_full, preferred_element_type=jnp.float32)

time: 314 us -> 174 us (0.55)
  other arithmetic: 84.6 us -> 9.14 us
  blocking collectives: 57 us -> 0 us
  Pallas kernels: 121 us -> 133 us
  matrix products: 33.4 us -> 22.6 us
  local copies, waits for them, and re-layouts: 17.6 us -> 8.53 us
    reduce_sum x2 -> x3, other arithmetic: 81.1 us -> 1.42 us  [the longest x1 0.86 us: neighbour_widths(): obs_square = jnp.sum(obs_float * obs_float, axis=1)]
    all_gather x2 -> x0, blocking collectives: 57 us -> none  [the longest x1 28.6 us: per_device(): obs_block = lax.all_gather(obs_summaries, COLS, axis=0, tiled=True)]
    reduce_sum x1 -> x0, local copies, waits for them, and re-layouts: 17.5 us -> none  [per_device(): jnp.sum((index_block[:, :, None] == sim_ids).astype(jnp.float32), axis=1)]
    pallas_call x0 -> x1, Pallas kernels: none -> 9.17 us  [col_gather(): pl.pallas_call(col_gather_kernel, out_shape=jax.ShapeDtypeStruct((n_col,)...]
    dot_general x1, matrix products: 20.5 us -> 13.4 us  [per_device(): jnp.dot(weight.astype(jnp.bfloat16), field_full, preferred_element_type=j...]
    gather x0 -> x1, local copies, waits for them, and re-layouts: none -> 6.19 us  [neighbour_widths(): near_rows = jnp.take(sims_full, index_rows, axis=0).astype(jnp.float32)]
    dot_general x1, matrix products: 12.9 us -> 8.16 us  [per_device(): lax.dot_general(obs_block, sims_full, (((1,), (1,)), ((), ())), preferred...]
where the time goes in v3:
time: 174 us; the launch traced here: 173 us
  Pallas kernels  133 us (76%)
  matrix products  22.6 us (13%)
  other arithmetic  9.14 us (5%)
  local copies, waits for them, and re-layouts  8.53 us (5%)
    pallas_call x1, Pallas kernels, ring_gather(): pl.pallas_call(functools.partial(ring_gather_kernel, n_z), out_shape=(jax...  124 us
    dot_general x1, matrix products, per_device(): jnp.dot(weight.astype(jnp.bfloat16), field_full, preferred_element_type=j...  13.4 us
    pallas_call x1, Pallas kernels, col_gather(): pl.pallas_call(col_gather_kernel, out_shape=jax.ShapeDtypeStruct((n_col,)...  9.17 us
    dot_general x1, matrix products, per_device(): lax.dot_general(obs_block, sims_full, (((1,), (1,)), ((), ())), preferred...  8.16 us
    gather x1, local copies, waits for them, and re-layouts, neighbour_widths(): near_rows = jnp.take(sims_full, index_rows, axis=0).astype(jnp.float32)  6.19 us

profile of v3, /device:TPU:8, one launch (start us, length us, event | category | flops | bytes accessed | tf_op | source)
XLA Modules:
  0.0 173.1 jit_solution(4506144997545800471)
XLA Ops:
  0.0 0.9 multiply_reduce_fusion.3
  0.9 0.7 compare_and_fusion
  1.6 0.1 copy.14
  1.7 0.7 compare_select_fusion
  2.4 0.1 copy.15
  2.5 0.1 reshape.43
  2.6 1.4 copy.13.nbr_ref
  4.0 123.6 %shard_map.46 = (bf16[32,256,1024]{2,1,0:T(8,128)(2,1)}, bf16[32,256,256]{2,1,0:T(8,128)(2,1)}, bf16[8,64,256]{2,1,0:T(8,128)(2,1)}, s32[8,64,16]{2,1,0:T(8,128)}) custom-call(bf16[256,1024]{1,0:T(8,128)(2,1)} %field_ref.1, bf16[256,256]{1,0:T(8,128)(2,1)} %sims_ref.1, bf16[64,256]{1,0:T(8,128)(2,1)} %obs_ref.1, s32[64,16]{1,0:T(8,128)} %copy.13.nbr_ref), custom_call_target="tpu_custom_call" | custom-call | tf_op jit(solution)/shard_map/pallas_call | solution.py:153
  127.5 1.1 multiply_reduce_fusion.2
  128.6 0.1 add.49
  128.7 3.3 %multiply_reduce_fusion = f32[32,256]{1,0:T(8,128)S(1)} fusion(bf16[32,256,256]{2,1,0:T(8,128)(2,1)} %get-tuple-element.9), kind=kLoop, calls=%fused_computation.4 | loop fusion | flops 6283264 | bytes 4227072 | tf_op jit(solution)/shard_map/reduce_sum | solution.py:251
  132.1 6.2 %gather_fusion = bf16[1024,256]{1,0:T(8,128)(2,1)S(1)} fusion(bf16[8192,256]{1,0:T(8,128)(2,1)} %bitcast.15, s32[1024]{0:T(1024)S(1)} %broadcast_clamp_fusion), kind=kCustom, calls=%fused_computation | custom fusion | bytes 1052672 | tf_op jit(solution)/shard_map/jit(_take)/gather | solution.py:232
  138.3 1.1 fusion.4
  139.4 0.4 multiply_reduce_fusion.1
  139.7 0.2 subtract_reduce_fusion
  139.9 0.5 add_bitcast_fusion.val_ref
  140.4 9.2 %shard_map.47 = f32[8,1,64]{2,1,0:T(1,128)} custom-call(f32[1,64]{1,0:T(1,128)} %add_bitcast_fusion.val_ref), custom_call_target="tpu_custom_call" | custom-call | tf_op jit(solution)/shard_map/pallas_call | solution.py:216
  149.6 0.5 broadcast.31
  150.1 1.3 reduce.5
  151.5 0.1 div.26
  151.6 8.2 %fusion.8 = (f32[512]{0:T(512)S(1)}, bf16[512,8192]{1,0:T(8,128)(2,1)S(1)}) fusion(f32[512]{0:T(512)S(1)} %div.26, bf16[512,256]{1,0:T(8,128)(2,1)} %bitcast.19, bf16[8192,256]{1,0:T(8,128)(2,1)} %bitcast.16, f32[8192]{0:T(1024)S(1)} %bitcast.22, f32[512]{0:T(512)S(1)} %add.49), kind=kOutput, calls=%fused_computation.19 | convolution fusion | flops 2176843264 | bytes 12883968 | tf_op jit(solution)/shard_map/dot_general | solution.py:254
  159.7 13.4 %divide_convert_fusion = bf16[512,1024]{1,0:T(8,128)(2,1)} fusion(bf16[8192,1024]{1,0:T(8,128)(2,1)} %bitcast.24, bf16[512,8192]{1,0:T(8,128)(2,1)S(1)} %get-tuple-element.12, f32[512]{0:T(512)S(1)} %get-tuple-element.11), kind=kOutput, calls=%fused_computation.5 | convolution fusion | flops 8590983168 | bytes 26216448 | tf_op jit(solution)/shard_map/dot_general | solution.py:260
  (2 shorter events, 0.0 us)

commit v4 on v3

--- a/solution.py
+++ b/solution.py
@@ -32,7 +32,7 @@
 
 def ring_gather_kernel(
     n_z, field_ref, sims_ref, obs_ref, nbr_ref, field_out, sims_out, obs_out, nbr_out,
-    send_sem, recv_sem, local_sem, col_send, col_recv,
+    send_sem, recv_sem, local_sem, col_send, col_recv, fan_send, fan_recv,
 ):
     z = lax.axis_index("z")
     yh = lax.axis_index("yh")
@@ -93,6 +93,25 @@
     n_fwd = n // 2
     n_bwd = n - 1 - n_fwd
     copies = []
+    part = sims_ref.shape[0] // (2 * n_x)
+    mine_rows = pl.ds(mine * part, part)
+
+    def fan_out(direction, step):
+        if direction == 0:
+            o = origin((pos - step + n) % n)
+        else:
+            o = origin((pos + step) % n)
+        for i, d in enumerate(peer_devs):
+            c = pltpu.make_async_remote_copy(
+                src_ref=sims_out.at[o, mine_rows],
+                dst_ref=sims_out.at[o, mine_rows],
+                send_sem=fan_send.at[direction, step - 1, i],
+                recv_sem=fan_recv.at[direction, step - 1, mine],
+                device_id=d,
+                device_id_type=MESH,
+            )
+            c.start()
+            copies.append(c)
 
     def hop(direction, step, target):
         if direction == 0:
@@ -101,12 +120,13 @@
             src_pos = (pos + step - 1) % n
         o = origin(src_pos)
         made = []
-        for k, (src_in, out) in enumerate(((field_ref, field_out), (sims_ref, sims_out))):
-            src = src_in if step == 1 else out.at[o]
+        for k, (src_in, out) in enumerate(((field_ref, field_out), (sims_ref.at[mine_rows], sims_out))):
+            dst = out.at[o] if k == 0 else out.at[o, mine_rows]
+            src = src_in if step == 1 else dst
             made.append(
                 pltpu.make_async_remote_copy(
                     src_ref=src,
-                    dst_ref=out.at[o],
+                    dst_ref=dst,
                     send_sem=send_sem.at[direction, k, step - 1],
                     recv_sem=recv_sem.at[direction, k, step - 1],
                     device_id=target,
@@ -123,14 +143,27 @@
             if prev[direction] is not None:
                 for c in prev[direction]:
                     c.wait_recv()
+                fan_out(direction, step - 1)
             made = hop(direction, step, target)
             for c in made:
                 c.start()
             copies.extend(made)
             prev[direction] = made
-    for direction in (0, 1):
+    for direction, count in ((0, n_fwd), (1, n_bwd)):
         for c in prev[direction]:
             c.wait_recv()
+        fan_out(direction, count)
+    for direction, count in ((0, n_fwd), (1, n_bwd)):
+        for step in range(1, count + 1):
+            for p in peers:
+                pltpu.make_async_remote_copy(
+                    src_ref=sims_out.at[0, mine_rows],
+                    dst_ref=sims_out.at[0, pl.ds(p * part, part)],
+                    send_sem=fan_send.at[direction, step - 1, 0],
+                    recv_sem=fan_recv.at[direction, step - 1, p],
+                    device_id=peer_devs[0],
+                    device_id_type=MESH,
+                ).wait_recv()
     for p in peers:
         for k, out in enumerate((obs_out, nbr_out)):
             pltpu.make_async_remote_copy(
@@ -166,6 +199,8 @@
             pltpu.SemaphoreType.DMA((4,)),
             pltpu.SemaphoreType.DMA((2, n_col - 1)),
             pltpu.SemaphoreType.DMA((2, n_col)),
+            pltpu.SemaphoreType.DMA((2, n_fwd, n_col - 1)),
+            pltpu.SemaphoreType.DMA((2, n_fwd, n_col)),
         ],
         compiler_params=pltpu.CompilerParams(collective_id=0, has_side_effects=True),
     )(field, sims, obs, nbr)

time: 174 us -> 211 us (1.21)
  Pallas kernels: 133 us -> 169 us
    pallas_call x1, Pallas kernels: 124 us -> 162 us  [ring_gather(): pl.pallas_call(functools.partial(ring_gather_kernel, n_z), out_shape=(jax...]
where the time goes in v4:
time: 211 us; the launch traced here: 210 us
  Pallas kernels  169 us (80%)
  matrix products  22.6 us (11%)
  other arithmetic  9.14 us (4%)
  local copies, waits for them, and re-layouts  8.71 us (4%)
    pallas_call x1, Pallas kernels, ring_gather(): pl.pallas_call(functools.partial(ring_gather_kernel, n_z), out_shape=(jax...  162 us
    dot_general x1, matrix products, per_device(): jnp.dot(weight.astype(jnp.bfloat16), field_full, preferred_element_type=j...  13.4 us
    dot_general x1, matrix products, per_device(): lax.dot_general(obs_block, sims_full, (((1,), (1,)), ((), ())), preferred...  8.15 us
    pallas_call x1, Pallas kernels, col_gather(): pl.pallas_call(col_gather_kernel, out_shape=jax.ShapeDtypeStruct((n_col,)...  7.32 us
    gather x1, local copies, waits for them, and re-layouts, neighbour_widths(): near_rows = jnp.take(sims_full, index_rows, axis=0).astype(jnp.float32)  6.37 us

profile of v4, /device:TPU:8, one launch (start us, length us, event | category | flops | bytes accessed | tf_op | source)
XLA Modules:
  0.0 209.6 jit_solution(8859028374968477267)
XLA Ops:
  0.0 0.9 multiply_reduce_fusion.3
  0.9 0.7 compare_and_fusion
  1.6 0.1 copy.14
  1.7 0.7 compare_select_fusion
  2.4 0.1 copy.15
  2.5 0.1 reshape.43
  2.6 1.4 copy.13.nbr_ref
  4.0 161.8 %shard_map.46 = (bf16[32,256,1024]{2,1,0:T(8,128)(2,1)}, bf16[32,256,256]{2,1,0:T(8,128)(2,1)}, bf16[8,64,256]{2,1,0:T(8,128)(2,1)}, s32[8,64,16]{2,1,0:T(8,128)}) custom-call(bf16[256,1024]{1,0:T(8,128)(2,1)} %field_ref.1, bf16[256,256]{1,0:T(8,128)(2,1)} %sims_ref.1, bf16[64,256]{1,0:T(8,128)(2,1)} %obs_ref.1, s32[64,16]{1,0:T(8,128)} %copy.13.nbr_ref), custom_call_target="tpu_custom_call" | custom-call | tf_op jit(solution)/shard_map/pallas_call | solution.py:186
  165.8 1.1 multiply_reduce_fusion.2
  166.9 0.1 add.49
  166.9 3.3 %multiply_reduce_fusion = f32[32,256]{1,0:T(8,128)S(1)} fusion(bf16[32,256,256]{2,1,0:T(8,128)(2,1)} %get-tuple-element.9), kind=kLoop, calls=%fused_computation.4 | loop fusion | flops 6283264 | bytes 4227072 | tf_op jit(solution)/shard_map/reduce_sum | solution.py:286
  170.3 6.4 %gather_fusion = bf16[1024,256]{1,0:T(8,128)(2,1)S(1)} fusion(bf16[8192,256]{1,0:T(8,128)(2,1)} %bitcast.15, s32[1024]{0:T(1024)S(1)} %broadcast_clamp_fusion), kind=kCustom, calls=%fused_computation | custom fusion | bytes 1052672 | tf_op jit(solution)/shard_map/jit(_take)/gather | solution.py:267
  176.7 1.1 fusion.4
  177.8 0.4 multiply_reduce_fusion.1
  178.2 0.2 subtract_reduce_fusion
  178.3 0.5 add_bitcast_fusion.val_ref
  178.9 7.3 %shard_map.47 = f32[8,1,64]{2,1,0:T(1,128)} custom-call(f32[1,64]{1,0:T(1,128)} %add_bitcast_fusion.val_ref), custom_call_target="tpu_custom_call" | custom-call | tf_op jit(solution)/shard_map/pallas_call | solution.py:251
  186.2 0.5 broadcast.31
  186.7 1.3 reduce.5
  188.1 0.1 div.26
  188.1 8.2 %fusion.8 = (f32[512]{0:T(512)S(1)}, bf16[512,8192]{1,0:T(8,128)(2,1)S(1)}) fusion(f32[512]{0:T(512)S(1)} %div.26, bf16[512,256]{1,0:T(8,128)(2,1)} %bitcast.19, bf16[8192,256]{1,0:T(8,128)(2,1)} %bitcast.16, f32[8192]{0:T(1024)S(1)} %bitcast.22, f32[512]{0:T(512)S(1)} %add.49), kind=kOutput, calls=%fused_computation.19 | convolution fusion | flops 2176843264 | bytes 12883968 | tf_op jit(solution)/shard_map/dot_general | solution.py:289
  196.3 13.4 %divide_convert_fusion = bf16[512,1024]{1,0:T(8,128)(2,1)} fusion(bf16[8192,1024]{1,0:T(8,128)(2,1)} %bitcast.24, bf16[512,8192]{1,0:T(8,128)(2,1)S(1)} %get-tuple-element.12, f32[512]{0:T(512)S(1)} %get-tuple-element.11), kind=kOutput, calls=%fused_computation.5 | convolution fusion | flops 8590983168 | bytes 26216448 | tf_op jit(solution)/shard_map/dot_general | solution.py:295
  (2 shorter events, 0.0 us)

commit v5 on v4

--- a/solution.py
+++ b/solution.py
@@ -137,18 +137,21 @@
 
     prev = {0: None, 1: None}
     for step in range(1, n_fwd + 1):
+        arrived = []
         for direction, count, target in ((0, n_fwd, right), (1, n_bwd, left)):
             if step > count:
                 continue
             if prev[direction] is not None:
                 for c in prev[direction]:
                     c.wait_recv()
-                fan_out(direction, step - 1)
+                arrived.append(direction)
             made = hop(direction, step, target)
             for c in made:
                 c.start()
             copies.extend(made)
             prev[direction] = made
+        for direction in arrived:
+            fan_out(direction, step - 1)
     for direction, count in ((0, n_fwd), (1, n_bwd)):
         for c in prev[direction]:
             c.wait_recv()

time: 211 us -> 209 us (level)
  no operation moved by 1% of the time
where the time goes in v5:
time: 209 us; the launch traced here: 208 us
  Pallas kernels  168 us (80%)
  matrix products  22.6 us (11%)
  other arithmetic  9.14 us (4%)
  local copies, waits for them, and re-layouts  8.71 us (4%)
    pallas_call x1, Pallas kernels, ring_gather(): pl.pallas_call(functools.partial(ring_gather_kernel, n_z), out_shape=(jax...  161 us
    dot_general x1, matrix products, per_device(): jnp.dot(weight.astype(jnp.bfloat16), field_full, preferred_element_type=j...  13.4 us
    dot_general x1, matrix products, per_device(): lax.dot_general(obs_block, sims_full, (((1,), (1,)), ((), ())), preferred...  8.15 us
    pallas_call x1, Pallas kernels, col_gather(): pl.pallas_call(col_gather_kernel, out_shape=jax.ShapeDtypeStruct((n_col,)...  6.94 us
    gather x1, local copies, waits for them, and re-layouts, neighbour_widths(): near_rows = jnp.take(sims_full, index_rows, axis=0).astype(jnp.float32)  6.37 us

profile of v5, /device:TPU:8, one launch (start us, length us, event | category | flops | bytes accessed | tf_op | source)
XLA Modules:
  0.0 208.3 jit_solution(1205712622429060839)
XLA Ops:
  0.0 0.9 multiply_reduce_fusion.3
  0.9 0.7 compare_and_fusion
  1.6 0.1 copy.14
  1.7 0.7 compare_select_fusion
  2.4 0.1 copy.15
  2.5 0.1 reshape.43
  2.6 1.4 copy.13.nbr_ref
  4.0 160.8 %shard_map.46 = (bf16[32,256,1024]{2,1,0:T(8,128)(2,1)}, bf16[32,256,256]{2,1,0:T(8,128)(2,1)}, bf16[8,64,256]{2,1,0:T(8,128)(2,1)}, s32[8,64,16]{2,1,0:T(8,128)}) custom-call(bf16[256,1024]{1,0:T(8,128)(2,1)} %field_ref.1, bf16[256,256]{1,0:T(8,128)(2,1)} %sims_ref.1, bf16[64,256]{1,0:T(8,128)(2,1)} %obs_ref.1, s32[64,16]{1,0:T(8,128)} %copy.13.nbr_ref), custom_call_target="tpu_custom_call" | custom-call | tf_op jit(solution)/shard_map/pallas_call | solution.py:189
  164.8 1.1 multiply_reduce_fusion.2
  165.9 0.1 add.49
  166.0 3.3 %multiply_reduce_fusion = f32[32,256]{1,0:T(8,128)S(1)} fusion(bf16[32,256,256]{2,1,0:T(8,128)(2,1)} %get-tuple-element.9), kind=kLoop, calls=%fused_computation.4 | loop fusion | flops 6283264 | bytes 4227072 | tf_op jit(solution)/shard_map/reduce_sum | solution.py:289
  169.3 6.4 %gather_fusion = bf16[1024,256]{1,0:T(8,128)(2,1)S(1)} fusion(bf16[8192,256]{1,0:T(8,128)(2,1)} %bitcast.15, s32[1024]{0:T(1024)S(1)} %broadcast_clamp_fusion), kind=kCustom, calls=%fused_computation | custom fusion | bytes 1052672 | tf_op jit(solution)/shard_map/jit(_take)/gather | solution.py:270
  175.7 1.1 fusion.4
  176.8 0.4 multiply_reduce_fusion.1
  177.2 0.2 subtract_reduce_fusion
  177.4 0.5 add_bitcast_fusion.val_ref
  177.9 6.9 %shard_map.47 = f32[8,1,64]{2,1,0:T(1,128)} custom-call(f32[1,64]{1,0:T(1,128)} %add_bitcast_fusion.val_ref), custom_call_target="tpu_custom_call" | custom-call | tf_op jit(solution)/shard_map/pallas_call | solution.py:254
  184.8 0.5 broadcast.31
  185.3 1.3 reduce.5
  186.7 0.1 div.26
  186.8 8.1 %fusion.8 = (f32[512]{0:T(512)S(1)}, bf16[512,8192]{1,0:T(8,128)(2,1)S(1)}) fusion(f32[512]{0:T(512)S(1)} %div.26, bf16[512,256]{1,0:T(8,128)(2,1)} %bitcast.19, bf16[8192,256]{1,0:T(8,128)(2,1)} %bitcast.16, f32[8192]{0:T(1024)S(1)} %bitcast.22, f32[512]{0:T(512)S(1)} %add.49), kind=kOutput, calls=%fused_computation.19 | convolution fusion | flops 2176843264 | bytes 12883968 | tf_op jit(solution)/shard_map/dot_general | solution.py:292
  194.9 13.4 %divide_convert_fusion = bf16[512,1024]{1,0:T(8,128)(2,1)} fusion(bf16[8192,1024]{1,0:T(8,128)(2,1)} %bitcast.24, bf16[512,8192]{1,0:T(8,128)(2,1)S(1)} %get-tuple-element.12, f32[512]{0:T(512)S(1)} %get-tuple-element.11), kind=kOutput, calls=%fused_computation.5 | convolution fusion | flops 8590983168 | bytes 26216448 | tf_op jit(solution)/shard_map/dot_general | solution.py:298
  (2 shorter events, 0.0 us)

commit v6 on v2

v6 whole, which is shorter than its diff:
```python
import functools

import jax
import jax.numpy as jnp
from jax import lax
from jax.experimental import pallas as pl
from jax.experimental.pallas import tpu as pltpu
from jax.sharding import Mesh
from jax.sharding import PartitionSpec as P

SHARPNESS = 32.0
EPSILON = 1e-06
ROWS = ("z", "yh", "core")
COLS = ("yl", "x")
MESH = pl.DeviceIdType.MESH


def ring_device(pos, n_z, lane):
    chip = pos // 2
    core = pos % 2
    start = lane * (n_z // 2)
    low = chip < n_z
    z = jnp.where(low, (start + chip) % n_z, (start + 2 * n_z - 1 - chip) % n_z)
    yh = jnp.where(low, 0, 1)
    return z, yh, core


def posterior_kernel(
    n_z, field_ref, sims_ref, sq_ref, obs_ref, nbr_ref, out_ref,
    fbuf, sbuf, qbuf, obuf, wbuf, numer, total, ns,
    send_sem, recv_sem, col_send, col_recv, wid_send, wid_recv,
):
    z = lax.axis_index("z")
    yh = lax.axis_index("yh")
    core = lax.axis_index("core")
    yl = lax.axis_index("yl")
    x = lax.axis_index("x")
    n = 4 * n_z
    n_col = obuf.shape[0]
    n_x = n_col // 2
    sim_dev = sims_ref.shape[0]
    start = yl * (n_z // 2)
    rel = (z - start + n_z) % n_z
    chip = jnp.where(yh == 0, rel, 2 * n_z - 1 - rel)
    pos = 2 * chip + core
    me = (z * 2 + yh) * 2 + core
    mine = yl * n_x + x
    peers = [(mine + d) % n_col for d in range(1, n_col)]
    peer_devs = [(z, yh, core, p // n_x, p % n_x) for p in peers]

    def dev(p):
        dz, dyh, dcore = ring_device(p, n_z, yl)
        return (dz, dyh, dcore, yl, x)

    def origin(p):
        dz, dyh, dcore = ring_device(p, n_z, yl)
        return (dz * 2 + dyh) * 2 + dcore

    right = dev((pos + 1) % n)
    left = dev((pos + n - 1) % n)

    barrier = pltpu.get_barrier_semaphore()
    for d in [left, right] + peer_devs:
        pl.semaphore_signal(barrier, inc=1, device_id=d, device_id_type=MESH)
    pl.semaphore_wait(barrier, 2 + len(peer_devs))

    copies = []
    for i, d in enumerate(peer_devs):
        c = pltpu.make_async_remote_copy(
            src_ref=obs_ref, dst_ref=obuf.at[mine], send_sem=col_send.at[i],
            recv_sem=col_recv.at[mine], device_id=d, device_id_type=MESH,
        )
        c.start()
        copies.append(c)

    n_fwd = n // 2
    n_bwd = n - 1 - n_fwd
    pairs = ((field_ref, fbuf), (sims_ref, sbuf), (sq_ref, qbuf))

    def hop(direction, step, target):
        if direction == 0:
            src_pos = (pos - step + 1 + n) % n
        else:
            src_pos = (pos + step - 1) % n
        o = origin(src_pos)
        made = []
        for k, (src_in, buf) in enumerate(pairs):
            src = src_in if step == 1 else buf.at[o]
            made.append(
                pltpu.make_async_remote_copy(
                    src_ref=src, dst_ref=buf.at[o],
                    send_sem=send_sem.at[direction, k, step - 1],
                    recv_sem=recv_sem.at[direction, k, step - 1],
                    device_id=target, device_id_type=MESH,
                )
            )
        return made

    obs_own = obs_ref[...]
    obs_own_f = obs_own.astype(jnp.float32)
    obs_own_sq = jnp.sum(obs_own_f * obs_own_f, axis=1, keepdims=True)
    nbr = nbr_ref[...]
    ns[...] = jnp.zeros_like(ns)

    def neighbour_sums(o, sims_blk, sq_blk):
        cross = lax.dot_general(
            obs_own, sims_blk, (((1,), (1,)), ((), ())), preferred_element_type=jnp.float32
        )
        dist = obs_own_sq + sq_blk - 2.0 * cross
        ids = lax.broadcasted_iota(jnp.int32, dist.shape, 1) + o * sim_dev
        counts = jnp.zeros(dist.shape, jnp.float32)
        for k in range(nbr.shape[1]):
            counts = counts + (nbr[:, k : k + 1] == ids).astype(jnp.float32)
        ns[...] += jnp.sum(counts * dist, axis=1, keepdims=True)

    fbuf[me] = field_ref[...]
    sbuf[me] = sims_ref[...]
    qbuf[me] = sq_ref[...]
    obuf[mine] = obs_own

    prev = {0: None, 1: None}
    for step in range(1, n_fwd + 1):
        arrived = []
        for direction, count, target in ((0, n_fwd, right), (1, n_bwd, left)):
            if step > count:
                continue
            if prev[direction] is not None:
                for c in prev[direction]:
                    c.wait_recv()
                arrived.append(direction)
            made = hop(direction, step, target)
            for c in made:
                c.start()
            copies.extend(made)
            prev[direction] = made
        if step == 1:
            neighbour_sums(me, sims_ref[...], sq_ref[...])
        for direction in arrived:
            got = (pos - step + 1 + n) % n if direction == 0 else (pos + step - 1) % n
            o = origin(got)
            neighbour_sums(o, sbuf[o], qbuf[o])
    for direction, count in ((0, n_fwd), (1, n_bwd)):
        for c in prev[direction]:
            c.wait_recv()
        got = (pos - count + n) % n if direction == 0 else (pos + count) % n
        o = origin(got)
        neighbour_sums(o, sbuf[o], qbuf[o])

    wbuf[mine] = ns[...] / nbr.shape[1] + EPSILON
    wid = []
    for i, d in enumerate(peer_devs):
        c = pltpu.make_async_remote_copy(
            src_ref=wbuf.at[mine], dst_ref=wbuf.at[mine], send_sem=wid_send.at[i],
            recv_sem=wid_recv.at[mine], device_id=d, device_id_type=MESH,
        )
        c.start()
        wid.append(c)
    for p in peers:
        pltpu.make_async_remote_copy(
            src_ref=obuf.at[p], dst_ref=obuf.at[p], send_sem=col_send.at[0],
            recv_sem=col_recv.at[p], device_id=peer_devs[0], device_id_type=MESH,
        ).wait_recv()
        pltpu.make_async_remote_copy(
            src_ref=wbuf.at[p], dst_ref=wbuf.at[p], send_sem=wid_send.at[0],
            recv_sem=wid_recv.at[p], device_id=peer_devs[0], device_id_type=MESH,
        ).wait_recv()
    for c in copies + wid:
        c.wait_send()

    rows = n_col * obs_ref.shape[0]
    obs_all = obuf[...].reshape(rows, obs_ref.shape[1])
    obs_all_f = obs_all.astype(jnp.float32)
    obs_sq = jnp.sum(obs_all_f * obs_all_f, axis=1, keepdims=True)
    width = wbuf[...].reshape(rows, 1)
    numer[...] = jnp.zeros_like(numer)
    total[...] = jnp.zeros_like(total)

    @pl.loop(0, n)
    def _(b):
        cross = lax.dot_general(
            obs_all, sbuf[b], (((1,), (1,)), ((), ())), preferred_element_type=jnp.float32
        )
        dist = obs_sq + qbuf[b] - 2.0 * cross
        weight = jnp.exp(-SHARPNESS * dist / width)
        total[...] += jnp.sum(weight, axis=1, keepdims=True)
        numer[...] += jnp.dot(weight.astype(jnp.bfloat16), fbuf[b], preferred_element_type=jnp.float32)

    out_ref[...] = (numer[...] / total[...]).astype(out_ref.dtype)


def posterior(field, sims, sq, obs, nbr, n_z, n_col):
    n = 4 * n_z
    n_fwd = n // 2
    rows = n_col * obs.shape[0]
    vmem = pltpu.VMEM
    return pl.pallas_call(
        functools.partial(posterior_kernel, n_z),
        out_shape=jax.ShapeDtypeStruct((rows, field.shape[1]), field.dtype),
        in_specs=[pl.BlockSpec(memory_space=vmem)] * 5,
        out_specs=pl.BlockSpec(memory_space=vmem),
        scratch_shapes=[
            vmem((n,) + field.shape, field.dtype),
            vmem((n,) + sims.shape, sims.dtype),
            vmem((n,) + sq.shape, sq.dtype),
            vmem((n_col,) + obs.shape, obs.dtype),
            vmem((n_col, obs.shape[0], 1), jnp.float32),
            vmem((rows, field.shape[1]), jnp.float32),
            vmem((rows, 1), jnp.float32),
            vmem((obs.shape[0], 1), jnp.float32),
            pltpu.SemaphoreType.DMA((2, 3, n_fwd)),
            pltpu.SemaphoreType.DMA((2, 3, n_fwd)),
            pltpu.SemaphoreType.DMA((n_col - 1,)),
            pltpu.SemaphoreType.DMA((n_col,)),
            pltpu.SemaphoreType.DMA((n_col - 1,)),
            pltpu.SemaphoreType.DMA((n_col,)),
        ],
        compiler_params=pltpu.CompilerParams(
            collective_id=0, has_side_effects=True, vmem_limit_bytes=60 * 1024 * 1024
        ),
    )(field, sims, sq, obs, nbr)


def per_device(n_z, obs_summaries, sim_summaries, neighbours, field):
    n_col = 2 * lax.psum(1, "x")
    sim_float = sim_summaries.astype(jnp.float32)
    sim_square = jnp.sum(sim_float * sim_float, axis=1).reshape(1, -1)
    return posterior(field, sim_summaries, sim_square, obs_summaries, neighbours, n_z, n_col)


def solution(mesh):
    n_row, n_col = mesh.devices.shape
    n_z = n_row // 4
    fine = Mesh(mesh.devices.reshape(n_z, 2, 2, 2, n_col // 2), ROWS + COLS)
    return jax.shard_map(
        functools.partial(per_device, n_z),
        mesh=fine,
        in_specs=(
            P(ROWS + COLS, None),
            P(ROWS, None),
            P(ROWS + COLS, None),
            P(ROWS, COLS),
        ),
        out_specs=P(ROWS, COLS),
        check_vma=False,
    )
```

time: 314 us -> 162 us (0.52)
  other arithmetic: 84.6 us -> 1.62 us
  blocking collectives: 57 us -> 0 us
  Pallas kernels: 121 us -> 156 us
  matrix products: 33.4 us -> 0 us
  local copies, waits for them, and re-layouts: 17.6 us -> 2.96 us
    reduce_sum x4 -> x1, other arithmetic: 84.6 us -> 1.62 us  [per_device(): sim_square = jnp.sum(sim_float * sim_float, axis=1).reshape(1, -1)]
    all_gather x2 -> x0, blocking collectives: 57 us -> none  [the longest x1 28.6 us: per_device(): obs_block = lax.all_gather(obs_summaries, COLS, axis=0, tiled=True)]
    pallas_call x1, Pallas kernels: 121 us -> 156 us  [posterior(): pl.pallas_call(functools.partial(posterior_kernel, n_z), out_shape=jax.Sh...]
    dot_general x2 -> x0, matrix products: 33.4 us -> none  [the longest x1 20.5 us: per_device(): jnp.dot(weight.astype(jnp.bfloat16), field_full, preferred_element_type=j...]
    reduce_sum x1 -> x0, local copies, waits for them, and re-layouts: 17.5 us -> none  [per_device(): jnp.sum((index_block[:, :, None] == sim_ids).astype(jnp.float32), axis=1)]
where the time goes in v6:
time: 162 us; the launch traced here: 160 us
  Pallas kernels  156 us (96%)
  local copies, waits for them, and re-layouts  2.96 us (2%)
  other arithmetic  1.62 us (1%)
    pallas_call x1, Pallas kernels, posterior(): pl.pallas_call(functools.partial(posterior_kernel, n_z), out_shape=jax.Sh...  156 us

profile of v6, /device:TPU:8, one launch (start us, length us, event | category | flops | bytes accessed | tf_op | source)
XLA Modules:
  0.0 160.4 jit_solution(1703471381046164952)
XLA Ops:
  0.0 0.0 copy-start
  0.0 1.6 %multiply_reduce_fusion = f32[256]{0:T(256)} fusion(bf16[256,256]{1,0:T(8,128)(2,1)} %sims_ref.1), kind=kLoop, calls=%fused_computation | loop fusion | flops 196352 | bytes 132096 | tf_op jit(solution)/shard_map/reduce_sum | solution.py:226
  1.6 0.0 copy-done
  1.6 0.7 copy.5.nbr_ref
  2.3 155.8 %shard_map.46 = bf16[512,1024]{1,0:T(8,128)(2,1)} custom-call(bf16[256,1024]{1,0:T(8,128)(2,1)} %field_ref.1, bf16[256,256]{1,0:T(8,128)(2,1)} %sims_ref.1, f32[1,256]{1,0:T(1,128)} %bitcast.1, bf16[64,256]{1,0:T(8,128)(2,1)} %obs_ref.1, s32[64,16]{1,0:T(8,128)} %copy.5.nbr_ref), custom_call_target="tpu_custom_call" | custom-call | tf_op jit(solution)/shard_map/pallas_call | solution.py:196
  158.1 2.3 %copy.7 = bf16[512,1024]{1,0:T(8,128)(2,1)} copy(bf16[512,1024]{1,0:T(8,128)(2,1)} %shard_map.46) | data formatting | bytes 2097152
Async XLA Ops:
  0.0 1.6 %copy-start = (s32[64,16]{0,1:T(8,128)S(1)}, s32[64,16]{0,1:T(8,128)}, u32[]{:S(2)}) copy-start(s32[64,16]{0,1:T(8,128)} %param.6) | copy-start | bytes 12292

commit v7 on v6

--- a/solution.py
+++ b/solution.py
@@ -27,7 +27,7 @@
 
 def posterior_kernel(
     n_z, field_ref, sims_ref, sq_ref, obs_ref, nbr_ref, out_ref,
-    fbuf, sbuf, qbuf, obuf, wbuf, numer, total, ns,
+    fbuf, sbuf, qbuf, obuf, wbuf, numer, total, ns, osq, wcol,
     send_sem, recv_sem, col_send, col_recv, wid_send, wid_recv,
 ):
     z = lax.axis_index("z")
@@ -75,25 +75,32 @@
 
     n_fwd = n // 2
     n_bwd = n - 1 - n_fwd
-    pairs = ((field_ref, fbuf), (sims_ref, sbuf), (sq_ref, qbuf))
-
-    def hop(direction, step, target):
+    count = {0: n_fwd, 1: n_bwd}
+    target = {0: right, 1: left}
+    field_pairs = ((0, field_ref, fbuf),)
+    sims_pairs = ((1, sims_ref, sbuf), (2, sq_ref, qbuf))
+
+    def src_pos(direction, step):
         if direction == 0:
-            src_pos = (pos - step + 1 + n) % n
-        else:
-            src_pos = (pos + step - 1) % n
-        o = origin(src_pos)
+            return (pos - step + 1 + n) % n
+        return (pos + step - 1) % n
+
+    def hop(pairs, direction, step):
+        o = origin(src_pos(direction, step))
         made = []
-        for k, (src_in, buf) in enumerate(pairs):
+        for k, src_in, buf in pairs:
             src = src_in if step == 1 else buf.at[o]
             made.append(
                 pltpu.make_async_remote_copy(
                     src_ref=src, dst_ref=buf.at[o],
                     send_sem=send_sem.at[direction, k, step - 1],
                     recv_sem=recv_sem.at[direction, k, step - 1],
-                    device_id=target, device_id_type=MESH,
+                    device_id=target[direction], device_id_type=MESH,
                 )
             )
+        for c in made:
+            c.start()
+        copies.extend(made)
         return made
 
     obs_own = obs_ref[...]
@@ -117,73 +124,100 @@
     sbuf[me] = sims_ref[...]
     qbuf[me] = sq_ref[...]
     obuf[mine] = obs_own
-
-    prev = {0: None, 1: None}
-    for step in range(1, n_fwd + 1):
-        arrived = []
-        for direction, count, target in ((0, n_fwd, right), (1, n_bwd, left)):
-            if step > count:
-                continue
-            if prev[direction] is not None:
-                for c in prev[direction]:
-                    c.wait_recv()
-                arrived.append(direction)
-            made = hop(direction, step, target)
-            for c in made:
-                c.start()
-            copies.extend(made)
-            prev[direction] = made
-        if step == 1:
-            neighbour_sums(me, sims_ref[...], sq_ref[...])
-        for direction in arrived:
-            got = (pos - step + 1 + n) % n if direction == 0 else (pos + step - 1) % n
-            o = origin(got)
-            neighbour_sums(o, sbuf[o], qbuf[o])
-    for direction, count in ((0, n_fwd), (1, n_bwd)):
-        for c in prev[direction]:
-            c.wait_recv()
-        got = (pos - count + n) % n if direction == 0 else (pos + count) % n
-        o = origin(got)
-        neighbour_sums(o, sbuf[o], qbuf[o])
-
-    wbuf[mine] = ns[...] / nbr.shape[1] + EPSILON
-    wid = []
-    for i, d in enumerate(peer_devs):
-        c = pltpu.make_async_remote_copy(
-            src_ref=wbuf.at[mine], dst_ref=wbuf.at[mine], send_sem=wid_send.at[i],
-            recv_sem=wid_recv.at[mine], device_id=d, device_id_type=MESH,
-        )
-        c.start()
-        wid.append(c)
-    for p in peers:
-        pltpu.make_async_remote_copy(
-            src_ref=obuf.at[p], dst_ref=obuf.at[p], send_sem=col_send.at[0],
-            recv_sem=col_recv.at[p], device_id=peer_devs[0], device_id_type=MESH,
-        ).wait_recv()
-        pltpu.make_async_remote_copy(
-            src_ref=wbuf.at[p], dst_ref=wbuf.at[p], send_sem=wid_send.at[0],
-            recv_sem=wid_recv.at[p], device_id=peer_devs[0], device_id_type=MESH,
-        ).wait_recv()
-    for c in copies + wid:
-        c.wait_send()
-
-    rows = n_col * obs_ref.shape[0]
-    obs_all = obuf[...].reshape(rows, obs_ref.shape[1])
-    obs_all_f = obs_all.astype(jnp.float32)
-    obs_sq = jnp.sum(obs_all_f * obs_all_f, axis=1, keepdims=True)
-    width = wbuf[...].reshape(rows, 1)
     numer[...] = jnp.zeros_like(numer)
     total[...] = jnp.zeros_like(total)
-
-    @pl.loop(0, n)
-    def _(b):
+    rows = n_col * obs_ref.shape[0]
+
+    state = {"f": {0: 0, 1: 0}, "s": {0: 0, 1: 0}, "pf": {0: None, 1: None}, "ps": {0: None, 1: None}}
+    pending = [me]
+    wid = []
+
+    def advance(kind, direction):
+        step = state[kind][direction] + 1
+        if step > count[direction]:
+            return
+        before = state["p" + kind][direction]
+        if before is not None:
+            for c in before:
+                c.wait_recv()
+            o = origin(src_pos(direction, step))
+            if kind == "f":
+                pending.append(o)
+            else:
+                neighbour_sums(o, sbuf[o], qbuf[o])
+        state["p" + kind][direction] = hop(field_pairs if kind == "f" else sims_pairs, direction, step)
+        state[kind][direction] = step
+
+    def finish(kind, direction):
+        for c in state["p" + kind][direction]:
+            c.wait_recv()
+        last = count[direction]
+        o = origin((pos - last + n) % n if direction == 0 else (pos + last) % n)
+        if kind == "f":
+            pending.append(o)
+        else:
+            neighbour_sums(o, sbuf[o], qbuf[o])
+
+    def share_widths():
+        for direction in (0, 1):
+            finish("s", direction)
+        wbuf[mine] = ns[...] / nbr.shape[1] + EPSILON
+        for i, d in enumerate(peer_devs):
+            c = pltpu.make_async_remote_copy(
+                src_ref=wbuf.at[mine], dst_ref=wbuf.at[mine], send_sem=wid_send.at[i],
+                recv_sem=wid_recv.at[mine], device_id=d, device_id_type=MESH,
+            )
+            c.start()
+            wid.append(c)
+        for p in peers:
+            pltpu.make_async_remote_copy(
+                src_ref=obuf.at[p], dst_ref=obuf.at[p], send_sem=col_send.at[0],
+                recv_sem=col_recv.at[p], device_id=peer_devs[0], device_id_type=MESH,
+            ).wait_recv()
+            pltpu.make_async_remote_copy(
+                src_ref=wbuf.at[p], dst_ref=wbuf.at[p], send_sem=wid_send.at[0],
+                recv_sem=wid_recv.at[p], device_id=peer_devs[0], device_id_type=MESH,
+            ).wait_recv()
+        obs_all_f = obuf[...].reshape(rows, obs_ref.shape[1]).astype(jnp.float32)
+        osq[...] = jnp.sum(obs_all_f * obs_all_f, axis=1, keepdims=True)
+        wcol[...] = wbuf[...].reshape(rows, 1)
+
+    def process(b):
+        obs_all = obuf[...].reshape(rows, obs_ref.shape[1])
         cross = lax.dot_general(
             obs_all, sbuf[b], (((1,), (1,)), ((), ())), preferred_element_type=jnp.float32
         )
-        dist = obs_sq + qbuf[b] - 2.0 * cross
-        weight = jnp.exp(-SHARPNESS * dist / width)
+        dist = osq[...] + qbuf[b] - 2.0 * cross
+        weight = jnp.exp(-SHARPNESS * dist / wcol[...])
         total[...] += jnp.sum(weight, axis=1, keepdims=True)
         numer[...] += jnp.dot(weight.astype(jnp.bfloat16), fbuf[b], preferred_element_type=jnp.float32)
+
+    ready = False
+    sims_rate = 2
+    per_step = 4
+    neighbour_sums(me, sims_ref[...], sq_ref[...])
+    for step in range(1, n_fwd + 1):
+        for direction in (0, 1):
+            advance("f", direction)
+        if state["s"][0] < count[0] or state["s"][1] < count[1]:
+            for _ in range(sims_rate):
+                for direction in (0, 1):
+                    advance("s", direction)
+        elif not ready:
+            share_widths()
+            ready = True
+        if ready:
+            for _ in range(per_step):
+                if pending:
+                    process(pending.pop(0))
+    for direction in (0, 1):
+        finish("f", direction)
+    if not ready:
+        share_widths()
+    for b in pending:
+        process(b)
+    for c in copies + wid:
+        c.wait_send()
 
     out_ref[...] = (numer[...] / total[...]).astype(out_ref.dtype)
 
@@ -207,6 +241,8 @@
             vmem((rows, field.shape[1]), jnp.float32),
             vmem((rows, 1), jnp.float32),
             vmem((obs.shape[0], 1), jnp.float32),
+            vmem((rows, 1), jnp.float32),
+            vmem((rows, 1), jnp.float32),
             pltpu.SemaphoreType.DMA((2, 3, n_fwd)),
             pltpu.SemaphoreType.DMA((2, 3, n_fwd)),
             pltpu.SemaphoreType.DMA((n_col - 1,)),

time: 162 us -> 166 us (1.025)
  Pallas kernels: 156 us -> 161 us
    pallas_call x1, Pallas kernels: 156 us -> 161 us  [posterior(): pl.pallas_call(functools.partial(posterior_kernel, n_z), out_shape=jax.Sh...]
where the time goes in v7:
time: 166 us; the launch traced here: 165 us
  Pallas kernels  161 us (97%)
  local copies, waits for them, and re-layouts  2.96 us (2%)
    pallas_call x1, Pallas kernels, posterior(): pl.pallas_call(functools.partial(posterior_kernel, n_z), out_shape=jax.Sh...  161 us

profile of v7, /device:TPU:8, one launch (start us, length us, event | category | flops | bytes accessed | tf_op | source)
XLA Modules:
  0.0 165.4 jit_solution(1201709017639726998)
XLA Ops:
  0.0 0.0 copy-start
  0.0 1.6 multiply_reduce_fusion
  1.6 0.0 copy-done
  1.6 0.7 copy.5.nbr_ref
  2.3 160.8 %shard_map.46 = bf16[512,1024]{1,0:T(8,128)(2,1)} custom-call(bf16[256,1024]{1,0:T(8,128)(2,1)} %field_ref.1, bf16[256,256]{1,0:T(8,128)(2,1)} %sims_ref.1, f32[1,256]{1,0:T(1,128)} %bitcast.1, bf16[64,256]{1,0:T(8,128)(2,1)} %obs_ref.1, s32[64,16]{1,0:T(8,128)} %copy.5.nbr_ref), custom_call_target="tpu_custom_call" | custom-call | tf_op jit(solution)/shard_map/pallas_call | solution.py:230
  163.1 2.3 %copy.7 = bf16[512,1024]{1,0:T(8,128)(2,1)} copy(bf16[512,1024]{1,0:T(8,128)(2,1)} %shard_map.46) | data formatting | bytes 2097152
Async XLA Ops:
  0.0 1.6 copy-start

commit v8 on v6

--- a/solution.py
+++ b/solution.py
@@ -27,7 +27,7 @@
 
 def posterior_kernel(
     n_z, field_ref, sims_ref, sq_ref, obs_ref, nbr_ref, out_ref,
-    fbuf, sbuf, qbuf, obuf, wbuf, numer, total, ns,
+    fbuf, sbuf, qbuf, obuf, wbuf, numer, wbig, total, ns,
     send_sem, recv_sem, col_send, col_recv, wid_send, wid_recv,
 ):
     z = lax.axis_index("z")
@@ -77,6 +77,11 @@
     n_bwd = n - 1 - n_fwd
     pairs = ((field_ref, fbuf), (sims_ref, sbuf), (sq_ref, qbuf))
 
+    def block(buf, o):
+        if buf is fbuf:
+            return fbuf.at[pl.ds(pl.multiple_of(o * sim_dev, sim_dev), sim_dev)]
+        return buf.at[o]
+
     def hop(direction, step, target):
         if direction == 0:
             src_pos = (pos - step + 1 + n) % n
@@ -85,10 +90,10 @@
         o = origin(src_pos)
         made = []
         for k, (src_in, buf) in enumerate(pairs):
-            src = src_in if step == 1 else buf.at[o]
+            src = src_in if step == 1 else block(buf, o)
             made.append(
                 pltpu.make_async_remote_copy(
-                    src_ref=src, dst_ref=buf.at[o],
+                    src_ref=src, dst_ref=block(buf, o),
                     send_sem=send_sem.at[direction, k, step - 1],
                     recv_sem=recv_sem.at[direction, k, step - 1],
                     device_id=target, device_id_type=MESH,
@@ -113,7 +118,7 @@
             counts = counts + (nbr[:, k : k + 1] == ids).astype(jnp.float32)
         ns[...] += jnp.sum(counts * dist, axis=1, keepdims=True)
 
-    fbuf[me] = field_ref[...]
+    fbuf[pl.ds(pl.multiple_of(me * sim_dev, sim_dev), sim_dev)] = field_ref[...]
     sbuf[me] = sims_ref[...]
     qbuf[me] = sq_ref[...]
     obuf[mine] = obs_own
@@ -172,8 +177,8 @@
     obs_all_f = obs_all.astype(jnp.float32)
     obs_sq = jnp.sum(obs_all_f * obs_all_f, axis=1, keepdims=True)
     width = wbuf[...].reshape(rows, 1)
-    numer[...] = jnp.zeros_like(numer)
     total[...] = jnp.zeros_like(total)
+    scale = -SHARPNESS / width
 
     @pl.loop(0, n)
     def _(b):
@@ -181,11 +186,15 @@
             obs_all, sbuf[b], (((1,), (1,)), ((), ())), preferred_element_type=jnp.float32
         )
         dist = obs_sq + qbuf[b] - 2.0 * cross
-        weight = jnp.exp(-SHARPNESS * dist / width)
+        weight = jnp.exp(dist * scale)
         total[...] += jnp.sum(weight, axis=1, keepdims=True)
-        numer[...] += jnp.dot(weight.astype(jnp.bfloat16), fbuf[b], preferred_element_type=jnp.float32)
-
-    out_ref[...] = (numer[...] / total[...]).astype(out_ref.dtype)
+        wbig[:, pl.ds(pl.multiple_of(b * sim_dev, sim_dev), sim_dev)] = weight.astype(jnp.bfloat16)
+
+    cols = numer.shape[1]
+    step = 256
+    for j in range(cols // step):
+        part = jnp.dot(wbig[...], fbuf[:, pl.ds(j * step, step)], preferred_element_type=jnp.float32)
+        out_ref[:, pl.ds(j * step, step)] = (part / total[...]).astype(out_ref.dtype)
 
 
 def posterior(field, sims, sq, obs, nbr, n_z, n_col):
@@ -199,12 +208,13 @@
         in_specs=[pl.BlockSpec(memory_space=vmem)] * 5,
         out_specs=pl.BlockSpec(memory_space=vmem),
         scratch_shapes=[
-            vmem((n,) + field.shape, field.dtype),
+            vmem((n * field.shape[0], field.shape[1]), field.dtype),
             vmem((n,) + sims.shape, sims.dtype),
             vmem((n,) + sq.shape, sq.dtype),
             vmem((n_col,) + obs.shape, obs.dtype),
             vmem((n_col, obs.shape[0], 1), jnp.float32),
             vmem((rows, field.shape[1]), jnp.float32),
+            vmem((rows, n * field.shape[0]), jnp.bfloat16),
             vmem((rows, 1), jnp.float32),
             vmem((obs.shape[0], 1), jnp.float32),
             pltpu.SemaphoreType.DMA((2, 3, n_fwd)),

time: 162 us -> 160 us (0.988)
  Pallas kernels: 156 us -> 154 us
    pallas_call x1, Pallas kernels: 156 us -> 154 us  [posterior(): pl.pallas_call(functools.partial(posterior_kernel, n_z), out_shape=jax.Sh...]
where the time goes in v8:
time: 160 us; the launch traced here: 158 us
  Pallas kernels  154 us (96%)
  local copies, waits for them, and re-layouts  2.96 us (2%)
  other arithmetic  1.62 us (1%)
    pallas_call x1, Pallas kernels, posterior(): pl.pallas_call(functools.partial(posterior_kernel, n_z), out_shape=jax.Sh...  154 us

profile of v8, /device:TPU:8, one launch (start us, length us, event | category | flops | bytes accessed | tf_op | source)
XLA Modules:
  0.0 158.4 jit_solution(2698001442493625671)
XLA Ops:
  0.0 0.0 copy-start
  0.0 1.6 %multiply_reduce_fusion = f32[256]{0:T(256)} fusion(bf16[256,256]{1,0:T(8,128)(2,1)} %sims_ref.1), kind=kLoop, calls=%fused_computation | loop fusion | flops 196352 | bytes 132096 | tf_op jit(solution)/shard_map/reduce_sum | solution.py:236
  1.6 0.0 copy-done
  1.6 0.7 copy.5.nbr_ref
  2.3 153.8 %shard_map.46 = bf16[512,1024]{1,0:T(8,128)(2,1)} custom-call(bf16[256,1024]{1,0:T(8,128)(2,1)} %field_ref.1, bf16[256,256]{1,0:T(8,128)(2,1)} %sims_ref.1, f32[1,256]{1,0:T(1,128)} %bitcast.1, bf16[64,256]{1,0:T(8,128)(2,1)} %obs_ref.1, s32[64,16]{1,0:T(8,128)} %copy.5.nbr_ref), custom_call_target="tpu_custom_call" | custom-call | tf_op jit(solution)/shard_map/pallas_call | solution.py:205
  156.1 2.3 %copy.7 = bf16[512,1024]{1,0:T(8,128)(2,1)} copy(bf16[512,1024]{1,0:T(8,128)(2,1)} %shard_map.46) | data formatting | bytes 2097152
Async XLA Ops:
  0.0 1.6 %copy-start = (s32[64,16]{0,1:T(8,128)S(1)}, s32[64,16]{0,1:T(8,128)}, u32[]{:S(2)}) copy-start(s32[64,16]{0,1:T(8,128)} %param.6) | copy-start | bytes 12292

commit v9 on v8

--- a/solution.py
+++ b/solution.py
@@ -27,7 +27,7 @@
 
 def posterior_kernel(
     n_z, field_ref, sims_ref, sq_ref, obs_ref, nbr_ref, out_ref,
-    fbuf, sbuf, qbuf, obuf, wbuf, numer, wbig, total, ns,
+    fbuf, sbuf, qbuf, obuf, wbuf, dbig, wbig, total, ns, osq,
     send_sem, recv_sem, col_send, col_recv, wid_send, wid_recv,
 ):
     z = lax.axis_index("z")
@@ -117,7 +117,13 @@
         for k in range(nbr.shape[1]):
             counts = counts + (nbr[:, k : k + 1] == ids).astype(jnp.float32)
         ns[...] += jnp.sum(counts * dist, axis=1, keepdims=True)
-
+        cross_all = lax.dot_general(
+            obuf[...].reshape(rows, obs_ref.shape[1]), sims_blk, (((1,), (1,)), ((), ())),
+            preferred_element_type=jnp.float32,
+        )
+        dbig[:, pl.ds(pl.multiple_of(o * sim_dev, sim_dev), sim_dev)] = osq[...] + sq_blk - 2.0 * cross_all
+
+    rows = n_col * obs_ref.shape[0]
     fbuf[pl.ds(pl.multiple_of(me * sim_dev, sim_dev), sim_dev)] = field_ref[...]
     sbuf[me] = sims_ref[...]
     qbuf[me] = sq_ref[...]
@@ -139,6 +145,13 @@
             copies.extend(made)
             prev[direction] = made
         if step == 1:
+            for p in peers:
+                pltpu.make_async_remote_copy(
+                    src_ref=obuf.at[p], dst_ref=obuf.at[p], send_sem=col_send.at[0],
+                    recv_sem=col_recv.at[p], device_id=peer_devs[0], device_id_type=MESH,
+                ).wait_recv()
+            obs_all_f = obuf[...].reshape(rows, obs_ref.shape[1]).astype(jnp.float32)
+            osq[...] = jnp.sum(obs_all_f * obs_all_f, axis=1, keepdims=True)
             neighbour_sums(me, sims_ref[...], sq_ref[...])
         for direction in arrived:
             got = (pos - step + 1 + n) % n if direction == 0 else (pos + step - 1) % n
@@ -162,35 +175,24 @@
         wid.append(c)
     for p in peers:
         pltpu.make_async_remote_copy(
-            src_ref=obuf.at[p], dst_ref=obuf.at[p], send_sem=col_send.at[0],
-            recv_sem=col_recv.at[p], device_id=peer_devs[0], device_id_type=MESH,
-        ).wait_recv()
-        pltpu.make_async_remote_copy(
             src_ref=wbuf.at[p], dst_ref=wbuf.at[p], send_sem=wid_send.at[0],
             recv_sem=wid_recv.at[p], device_id=peer_devs[0], device_id_type=MESH,
         ).wait_recv()
     for c in copies + wid:
         c.wait_send()
 
-    rows = n_col * obs_ref.shape[0]
-    obs_all = obuf[...].reshape(rows, obs_ref.shape[1])
-    obs_all_f = obs_all.astype(jnp.float32)
-    obs_sq = jnp.sum(obs_all_f * obs_all_f, axis=1, keepdims=True)
     width = wbuf[...].reshape(rows, 1)
     total[...] = jnp.zeros_like(total)
     scale = -SHARPNESS / width
 
     @pl.loop(0, n)
     def _(b):
-        cross = lax.dot_general(
-            obs_all, sbuf[b], (((1,), (1,)), ((), ())), preferred_element_type=jnp.float32
-        )
-        dist = obs_sq + qbuf[b] - 2.0 * cross
+        dist = dbig[:, pl.ds(pl.multiple_of(b * sim_dev, sim_dev), sim_dev)]
         weight = jnp.exp(dist * scale)
         total[...] += jnp.sum(weight, axis=1, keepdims=True)
         wbig[:, pl.ds(pl.multiple_of(b * sim_dev, sim_dev), sim_dev)] = weight.astype(jnp.bfloat16)
 
-    cols = numer.shape[1]
+    cols = out_ref.shape[1]
     step = 256
     for j in range(cols // step):
         part = jnp.dot(wbig[...], fbuf[:, pl.ds(j * step, step)], preferred_element_type=jnp.float32)
@@ -213,10 +215,11 @@
             vmem((n,) + sq.shape, sq.dtype),
             vmem((n_col,) + obs.shape, obs.dtype),
             vmem((n_col, obs.shape[0], 1), jnp.float32),
-            vmem((rows, field.shape[1]), jnp.float32),
+            vmem((rows, n * field.shape[0]), jnp.float32),
             vmem((rows, n * field.shape[0]), jnp.bfloat16),
             vmem((rows, 1), jnp.float32),
             vmem((obs.shape[0], 1), jnp.float32),
+            vmem((rows, 1), jnp.float32),
             pltpu.SemaphoreType.DMA((2, 3, n_fwd)),
             pltpu.SemaphoreType.DMA((2, 3, n_fwd)),
             pltpu.SemaphoreType.DMA((n_col - 1,)),

time: 160 us -> 153 us (0.956)
  Pallas kernels: 154 us -> 148 us
    pallas_call x1, Pallas kernels: 154 us -> 148 us  [posterior(): pl.pallas_call(functools.partial(posterior_kernel, n_z), out_shape=jax.Sh...]
where the time goes in v9:
time: 153 us
  Pallas kernels  148 us (97%)
  local copies, waits for them, and re-layouts  2.96 us (2%)
  other arithmetic  1.62 us (1%)
    pallas_call x1, Pallas kernels, posterior(): pl.pallas_call(functools.partial(posterior_kernel, n_z), out_shape=jax.Sh...  148 us

profile of v9, /device:TPU:8, one launch (start us, length us, event | category | flops | bytes accessed | tf_op | source)
XLA Modules:
  0.0 152.8 jit_solution(4175884495740516271)
XLA Ops:
  0.0 0.0 copy-start
  0.0 1.6 %multiply_reduce_fusion = f32[256]{0:T(256)} fusion(bf16[256,256]{1,0:T(8,128)(2,1)} %sims_ref.1), kind=kLoop, calls=%fused_computation | loop fusion | flops 196352 | bytes 132096 | tf_op jit(solution)/shard_map/reduce_sum | solution.py:239
  1.6 0.0 copy-done
  1.6 0.7 copy.5.nbr_ref
  2.3 148.2 %shard_map.46 = bf16[512,1024]{1,0:T(8,128)(2,1)} custom-call(bf16[256,1024]{1,0:T(8,128)(2,1)} %field_ref.1, bf16[256,256]{1,0:T(8,128)(2,1)} %sims_ref.1, f32[1,256]{1,0:T(1,128)} %bitcast.1, bf16[64,256]{1,0:T(8,128)(2,1)} %obs_ref.1, s32[64,16]{1,0:T(8,128)} %copy.5.nbr_ref), custom_call_target="tpu_custom_call" | custom-call | tf_op jit(solution)/shard_map/pallas_call | solution.py:207
  150.5 2.3 %copy.7 = bf16[512,1024]{1,0:T(8,128)(2,1)} copy(bf16[512,1024]{1,0:T(8,128)(2,1)} %shard_map.46) | data formatting | bytes 2097152
Async XLA Ops:
  0.0 1.6 %copy-start = (s32[64,16]{0,1:T(8,128)S(1)}, s32[64,16]{0,1:T(8,128)}, u32[]{:S(2)}) copy-start(s32[64,16]{0,1:T(8,128)} %param.6) | copy-start | bytes 12292
